TPU v7x, 32 devices: a whole 2x2x4 slice. The times are simulated.
32 devices in a mesh: dp: 8 (over y, x, core), ctx: 4 (over z).
Axes of the slice: x: 2, y: 2, z: 4, core: 2. Of those that a mesh axis runs over, the one named last changes fastest.
Arguments:
- inputs: bfloat16 [8, 512, 2048], P('dp', 'ctx'), may hold values from -6 to 6
- segment: int32 [8, 512], P('dp', 'ctx'), may hold values from 0 to 3, as said below
- w_qkv: bfloat16 [2048, 6144], P(('dp', 'ctx')), may hold values from -0.125 to 0.125
- w_out: bfloat16 [2048, 2048], P(('dp', 'ctx')), may hold values from -0.125 to 0.125
- w_gate: bfloat16 [2048, 8192], P('dp', 'ctx'), may hold values from -0.125 to 0.125
- w_up: bfloat16 [2048, 8192], P('dp', 'ctx'), may hold values from -0.125 to 0.125
- w_down_t: bfloat16 [2048, 8192], P('dp', 'ctx'), may hold values from -0.0625 to 0.0625
- gains: float32 [4, 2048], replicated, may hold values from 0.25 to 1.75
- cotangent: bfloat16 [8, 512, 2048], P('dp', 'ctx'), may hold values from -6 to 6
Outputs:
- output: bfloat16 [8, 512, 2048], P('dp', 'ctx')
- input_grad: float32 [8, 512, 2048], P('dp', 'ctx')
- grad_qkv: float32 [2048, 6144], P(('dp', 'ctx'))
- grad_out: float32 [2048, 2048], P(('dp', 'ctx'))
- grad_gate: float32 [2048, 8192], P('dp', 'ctx')
- grad_up: float32 [2048, 8192], P('dp', 'ctx')
- grad_down_t: float32 [2048, 8192], P('dp', 'ctx')
- grad_gains: float32 [4, 2048], replicated
Inputs may be any that keep to these rules, and one draw needn't show every extreme that they name: `segment`: in every sequence ids 1, 2 and 3 mark three documents in this order, each of one position or more, and 0 marks padding, one position or more at the sequence's end.
All inputs are finite; a program needn't handle non-finite values.
Results may differ from a plain program's by a relative error of at most 0.015.
Values may be sent and summed in bfloat16 or wider, within the bound.
A program may use at most 704 MiB of HBM per device.

v0:
```python
import functools

import jax
import jax.numpy as jnp
from jax import lax
from jax.experimental import pallas as pl
from jax.experimental.pallas import tpu as pltpu
from jax.sharding import Mesh
from jax.sharding import PartitionSpec as P

HEAD_DIM = 128
EPS = 1e-06
ROPE_BASE = 500000.0
F32 = jnp.float32
BF16 = jnp.bfloat16
GROUP = ("core", "ctx")
ALL = ("chip", "core", "ctx")


PIECE = 32
SUM_PIECE = 32
PASS_AT = 1
LATE_TICK = 2
PASS_TICK = 4
LAGJ = 1
MESH_ID = pl.DeviceIdType.MESH


def row_factor(values):
    return lax.rsqrt(jnp.mean(values * values, axis=-1, keepdims=True) + EPS)


def row_norm_back(values, gain, grad):
    factor = row_factor(values)
    normed = values * factor
    scaled = gain * grad
    back = factor * (scaled - normed * jnp.mean(scaled * normed, axis=-1, keepdims=True))
    return back, jnp.sum(grad * normed, axis=0, keepdims=True)


def after_projected(total, ins, outs, rows):
    tokens, gains = ins
    residual_out, projected_out = outs
    projected_out[rows, :] = total
    gain = gains[2:3, :]
    residual = tokens[rows, :].astype(F32) + total * row_factor(total) * gain
    residual_out[rows, :] = residual
    return residual


def after_feed(total, ins, outs, rows):
    residual, cotangent, gains = ins
    output, gain_out = outs
    gain = gains[3:4, :]
    normed = total * row_factor(total) * gain
    output[rows, :] = (residual[rows, :] + normed).astype(BF16)
    back, term = row_norm_back(total, gain, cotangent[rows, :].astype(F32))
    gain_out[...] += term
    return back


def after_back(total, ins, outs, rows):
    projected, cotangent, gains = ins
    grad_out, gain_out = outs
    grad = cotangent[rows, :].astype(F32) + total
    grad_out[rows, :] = grad
    back, term = row_norm_back(projected[rows, :], gains[2:3, :], grad)
    gain_out[...] += term
    return back


def after_input(total, ins, outs, rows):
    (grad,), (result,) = ins, outs
    result[rows, :] = grad[rows, :] + total
    return None


def pass_tokens(total, ins, outs, rows):
    return ins[0][rows, :]


class Exchange:
    def __init__(self, spans, rows, width, piece, reduce, spread, row_fn, n_in, n_out, gain, extra=None):
        self.extra = extra
        self.spans, self.rows, self.width, self.piece = spans, rows, width, piece
        self.reduce, self.spread, self.row_fn = reduce, spread, row_fn
        self.n_in, self.n_out, self.gain = n_in, n_out, gain
        self.count = rows // piece

    def scratch(self):
        spans, count = self.spans, self.count
        block = pltpu.VMEM((spans * self.rows, self.width), BF16)
        sems = pltpu.SemaphoreType.DMA((spans, count))
        items = []
        if self.reduce:
            items += [block] * 4 + [pltpu.SemaphoreType.DMA] + [sems] * 6
        if self.spread:
            items += [pltpu.VMEM((2 * spans * self.rows, self.width), BF16)]
            items += [sems] * 7 + [pltpu.SemaphoreType.DMA]
        if self.extra is not None:
            items += self.extra.scratch()
        return items

    def body(self, *refs):
        spans, rows, piece, count = self.spans, self.rows, self.piece, self.count
        refs = list(refs)
        take = lambda n: [refs.pop(0) for _ in range(n)]
        partial = take(1)[0] if self.reduce else None
        ins = take(self.n_in)
        extra = self.extra
        if extra is not None:
            extra.ins = take(extra.n_in)
        outs = take(self.n_out)
        if extra is not None:
            extra.outs = take(extra.n_out)
        gathered = take(1)[0] if self.spread else None
        if self.reduce:
            own, near, from_left, from_right = take(4)
            (load_sem,) = take(1)
            near_send, near_recv, right_send, right_recv, left_send, left_recv = take(6)
        if self.spread:
            (held,) = take(1)
            fwd_send, fwd_recv, bwd_send, bwd_recv, own_send, side_send, side_recv = take(7)
            (store_sem,) = take(1)
        if extra is not None:
            extra.held = refs
        core = lax.axis_index("core")
        place = lax.axis_index("ctx")
        other = 1 - core
        has_left = place > 0
        has_right = place < spans - 1

        def at(block, k):
            return pl.ds(pl.multiple_of(block * rows + k * piece, piece), piece)

        def held_at(seq, block, k):
            return pl.ds(pl.multiple_of((seq * spans + block) * rows + k * piece, piece), piece)

        def remote(src, dst, send, recv, **device):
            return pltpu.make_async_remote_copy(
                src_ref=src, dst_ref=dst, send_sem=send, recv_sem=recv,
                device_id=device, device_id_type=MESH_ID,
            )

        barrier = pltpu.get_barrier_semaphore()
        if extra is not None:
            if not extra.met:
                meet_all(spans)
        else:
            pl.semaphore_signal(barrier, 1, device_id={"core": other}, device_id_type=MESH_ID)

            @pl.when(has_left)
            def _():
                pl.semaphore_signal(barrier, 1, device_id={"ctx": place - 1}, device_id_type=MESH_ID)

            @pl.when(has_right)
            def _():
                pl.semaphore_signal(barrier, 1, device_id={"ctx": place + 1}, device_id_type=MESH_ID)

            pl.semaphore_wait(barrier, 1 + has_left.astype(jnp.int32) + has_right.astype(jnp.int32))

        if self.gain is not None:
            outs[self.gain][...] = jnp.zeros_like(outs[self.gain])

        def near_copy(d, k):
            return remote(
                partial.at[held_at(other, d, k)], near.at[at(d, k)],
                near_send.at[d, k], near_recv.at[d, k], core=other,
            )

        def right_copy(d, k):
            return remote(
                own.at[at(d, k)], from_left.at[at(d, k)],
                right_send.at[d, k], right_recv.at[d, k], ctx=place + 1,
            )

        def left_copy(d, k):
            return remote(
                own.at[at(d, k)], from_right.at[at(d, k)],
                left_send.at[d, k], left_recv.at[d, k], ctx=place - 1,
            )

        def fwd_copy(o, k, send):
            where = held_at(core, o, k)
            return remote(held.at[where], held.at[where], send, fwd_recv.at[o, k], ctx=place + 1)

        def bwd_copy(o, k, send):
            where = held_at(core, o, k)
            return remote(held.at[where], held.at[where], send, bwd_recv.at[o, k], ctx=place - 1)

        def side_copy(o, k):
            where = held_at(core, o, k)
            return remote(held.at[where], held.at[where], side_send.at[o, k], side_recv.at[o, k], core=other)

        if extra is not None:
            extra.start()
        if self.reduce:
            load = pltpu.make_async_copy(
                partial.at[pl.ds(pl.multiple_of(core * spans * rows, rows), spans * rows)], own, load_sem
            )
            load.start()

            @pl.loop(0, count)
            def _(k):
                for j in range(spans):
                    near_copy(j, k).start()

            load.wait()

        def base(d, k):
            near_copy(d, k).wait_recv()
            return own[at(d, k), :].astype(F32) + near[at(d, k), :].astype(F32)

        def pass_on(d, k, arrived, copy, later):
            value = base(d, k)

            @pl.when(later)
            def _():
                copy(d, k).wait_recv()

            before = arrived[at(d, k), :].astype(F32)
            value = value + jnp.where(later, before, jnp.zeros_like(before))
            own[at(d, k), :] = value.astype(BF16)
            copy(d, k).start()

        def pass_right(k):
            for d in range(spans - 1, 0, -1):

                @pl.when(d > place)
                def _():
                    pass_on(d, k, from_left, right_copy, has_left)

        def pass_left(k):
            for d in range(spans - 1):

                @pl.when(d < place)
                def _():
                    pass_on(d, k, from_right, left_copy, has_right)

        def finish_step(k):
            total = None
            if self.reduce:
                total = base(place, k)

                @pl.when(has_left)
                def _():
                    right_copy(place, k).wait_recv()

                @pl.when(has_right)
                def _():
                    left_copy(place, k).wait_recv()

                zero = jnp.zeros_like(total)
                total = total + jnp.where(has_left, from_left[at(place, k), :].astype(F32), zero)
                total = total + jnp.where(has_right, from_right[at(place, k), :].astype(F32), zero)
            own_rows = pl.ds(pl.multiple_of(k * piece, piece), piece)
            result = self.row_fn(total, ins, outs, own_rows)
            if self.spread:
                held[held_at(core, place, k), :] = result.astype(BF16)

                @pl.when(has_right)
                def _():
                    fwd_copy(place, k, fwd_send.at[place, k]).start()

                @pl.when(has_left)
                def _():
                    bwd_copy(place, k, bwd_send.at[place, k]).start()

                side_copy(place, k).start()

        def relay_step(k, j):
            if True:

                @pl.when(place - j >= 0)
                def _():
                    fwd_copy(place - j, k, fwd_send.at[place - j, k]).wait_recv()

                    @pl.when(has_right)
                    def _():
                        fwd_copy(place - j, k, fwd_send.at[place - j, k]).start()

                    side_copy(place - j, k).start()

                @pl.when(place + j < spans)
                def _():
                    bwd_copy(place + j, k, bwd_send.at[place + j, k]).wait_recv()

                    @pl.when(has_left)
                    def _():
                        bwd_copy(place + j, k, bwd_send.at[place + j, k]).start()

                    side_copy(place + j, k).start()

        lag = spans - 1 if self.reduce else 0

        def due(k, run):
            @pl.when(jnp.logical_and(k >= 0, k < count))
            def _():
                run(k)

        @pl.loop(0, count + lag + (LAGJ * (spans - 1) if self.spread else 0))
        def _(t):
            if self.reduce:
                due(t - place, pass_right)
                due(t - (spans - 1 - place), pass_left)
                due(t - jnp.maximum(place, spans - 1 - place), finish_step)
            else:

                @pl.when(t == 0)
                def _():
                    for k in range(count):
                        finish_step(k)

            if self.spread:
                for j in range(1, spans):
                    after = t - lag - j * LAGJ

                    @pl.when(jnp.logical_and(after >= 0, after < count))
                    def _():
                        relay_step(after, j)
            if extra is not None:
                extra.tick(t)

        if extra is not None:
            extra.finish(count + lag + (LAGJ * (spans - 1) if self.spread else 0))
        if self.spread:

            @pl.loop(0, count)
            def _(k):
                for o in range(spans):
                    side_copy(o, k).wait_recv()

            store = pltpu.make_async_copy(held, gathered, store_sem)
            store.start()

        @pl.loop(0, count)
        def _(k):
            for d in range(spans):
                if self.reduce:
                    near_copy(d, k).wait_send()

                    @pl.when(d > place)
                    def _():
                        right_copy(d, k).wait_send()

                    @pl.when(d < place)
                    def _():
                        left_copy(d, k).wait_send()

                if self.spread:
                    side_copy(d, k).wait_send()

                    @pl.when(jnp.logical_and(d <= place, has_right))
                    def _():
                        fwd_copy(d, k, fwd_send.at[d, k]).wait_send()

                    @pl.when(jnp.logical_and(d >= place, has_left))
                    def _():
                        bwd_copy(d, k, bwd_send.at[d, k]).wait_send()

        if self.spread:
            store.wait()


def owner_of(chip, core, place, spans):
    member = core * spans + place
    return member // 2, lax.rem(member, 2), chip


def summer_of(chip, core, place, spans):
    member = chip * 2 + core
    return place, member // spans, lax.rem(member, spans)


def stays(chip, core, place, spans):
    to_chip, to_core, to_place = owner_of(chip, core, place, spans)
    return jnp.logical_and(to_chip == chip, jnp.logical_and(to_core == core, to_place == place))


def meet_all(spans):
    greet_all(spans, False)
    wait_all(spans, False)


def greet_all(spans, moves):
    chips = lax.axis_size("chip")
    barrier = pltpu.get_barrier_semaphore()
    chip = lax.axis_index("chip")
    core = lax.axis_index("core")
    place = lax.axis_index("ctx")
    for s in range(1, chips):
        pl.semaphore_signal(
            barrier, 1, device_id={"chip": lax.rem(chip + s, chips)}, device_id_type=MESH_ID
        )
    for s in range(1, 2 * spans):
        to_core, to_place = step_member(core, place, s, spans)
        pl.semaphore_signal(
            barrier, 1, device_id={"core": to_core, "ctx": to_place}, device_id_type=MESH_ID
        )
    if moves:

        @pl.when(jnp.logical_not(stays(chip, core, place, spans)))
        def _():
            for find in (owner_of, summer_of):
                to_chip, to_core, to_place = find(chip, core, place, spans)
                pl.semaphore_signal(
                    barrier, 1, device_id={"chip": to_chip, "core": to_core, "ctx": to_place}, device_id_type=MESH_ID
                )


def wait_all(spans, moves):
    count = lax.axis_size("chip") - 1 + 2 * spans - 1
    if moves:
        here = stays(lax.axis_index("chip"), lax.axis_index("core"), lax.axis_index("ctx"), spans)
        count = count + 2 * jnp.logical_not(here).astype(jnp.int32)
    pl.semaphore_wait(pltpu.get_barrier_semaphore(), count)


def step_member(core, place, s, spans):
    return lax.rem(core + s % 2, 2), lax.rem(place + s // 2, spans)


def meet_other_core():
    barrier = pltpu.get_barrier_semaphore()
    other = 1 - lax.axis_index("core")
    pl.semaphore_signal(barrier, 1, device_id={"core": other}, device_id_type=MESH_ID)
    pl.semaphore_wait(barrier, 1)


def split_body(gate, up, down, gate_up_out, down_out, held, load_sem, store_sem, send_sem, recv_sem):
    core = lax.axis_index("core")
    other = 1 - core
    rows, width = gate.shape
    half = width // 2
    where = pl.ds(pl.multiple_of(core * rows, rows), rows)
    places = [gate_up_out.at[where, :half], gate_up_out.at[where, half:], down_out.at[where, :]]
    mine = pl.ds(pl.multiple_of(core * half, half), half)
    theirs = pl.ds(pl.multiple_of(other * half, half), half)
    loads = [
        pltpu.make_async_copy(a.at[:, mine], held.at[i], load_sem.at[i]) for i, a in enumerate((gate, up, down))
    ]
    for load in loads:
        load.start()
    meet_other_core()
    sends = [
        pltpu.make_async_remote_copy(
            src_ref=a.at[:, theirs], dst_ref=places[i], send_sem=send_sem.at[i], recv_sem=recv_sem.at[i],
            device_id={"core": other}, device_id_type=MESH_ID,
        )
        for i, a in enumerate((gate, up, down))
    ]
    for send in sends:
        send.start()
    stores = [pltpu.make_async_copy(held.at[i], places[i], store_sem.at[i]) for i in range(3)]
    for load, store in zip(loads, stores):
        load.wait()
        store.start()
    for store, send in zip(stores, sends):
        store.wait()
        send.wait()


def split_columns(gate, up, down):
    rows, width = gate.shape
    hbm = pl.BlockSpec(memory_space=pl.ANY)
    three = pltpu.SemaphoreType.DMA((3,))
    return pl.pallas_call(
        split_body,
        out_shape=[
            jax.ShapeDtypeStruct((2 * rows, width), BF16),
            jax.ShapeDtypeStruct((2 * rows, width // 2), BF16),
        ],
        in_specs=[hbm] * 3,
        out_specs=[hbm] * 2,
        scratch_shapes=[pltpu.VMEM((3, rows, width // 2), BF16)] + [three] * 4,
        compiler_params=pltpu.CompilerParams(collective_id=6, has_side_effects=True, vmem_limit_bytes=8 << 20),
        name="split_columns",
    )(gate, up, down)


def join_body(gate, up, down, gate_out, up_out, down_out, arrived, send_sem, recv_sem):
    core = lax.axis_index("core")
    other = 1 - core
    rows, width = gate_out.shape
    half = width // 2
    meet_other_core()
    theirs = pl.ds(pl.multiple_of(other * rows, rows), rows)
    pairs = ((gate, gate_out), (up, up_out), (down, down_out))
    sends = [
        pltpu.make_async_remote_copy(
            src_ref=a.at[theirs], dst_ref=arrived.at[i], send_sem=send_sem.at[i], recv_sem=recv_sem.at[i],
            device_id={"core": other}, device_id_type=MESH_ID,
        )
        for i, (a, _) in enumerate(pairs)
    ]
    for send in sends:
        send.start()
    mine = pl.ds(pl.multiple_of(core * half, half), half)
    far = pl.ds(pl.multiple_of(other * half, half), half)
    step = 16

    def rows_at(i, base):
        return pl.ds(pl.multiple_of(base + i * step, step), step)

    @pl.loop(0, rows // step)
    def _(i):
        for a, b in pairs:
            b[rows_at(i, 0), mine] = a[rows_at(i, core * rows), :].astype(F32)

    for send in sends:
        send.wait()

    @pl.loop(0, rows // step)
    def _(i):
        for n, (_, b) in enumerate(pairs):
            b[rows_at(i, 0), far] = arrived[n, rows_at(i, 0), :].astype(F32)


def join_columns(gate, up, down):
    rows, half = gate.shape[0] // 2, gate.shape[1]
    vmem = pl.BlockSpec(memory_space=pltpu.VMEM)
    three = pltpu.SemaphoreType.DMA((3,))
    return pl.pallas_call(
        join_body,
        out_shape=[jax.ShapeDtypeStruct((rows, 2 * half), F32)] * 3,
        in_specs=[vmem] * 3,
        out_specs=[vmem] * 3,
        scratch_shapes=[pltpu.VMEM((3, rows, half), BF16), three, three],
        compiler_params=pltpu.CompilerParams(collective_id=7, has_side_effects=True, vmem_limit_bytes=32 << 20),
        name="join_columns",
    )(gate, up, down)


class Extra:
    met = False

    def remote(self, src, dst, send, recv, **device):
        return pltpu.make_async_remote_copy(
            src_ref=src, dst_ref=dst, send_sem=send, recv_sem=recv,
            device_id=device, device_id_type=MESH_ID,
        )

    def locate(self):
        self.chip = lax.axis_index("chip")
        self.core = lax.axis_index("core")
        self.place = lax.axis_index("ctx")
        self.me = self.core * self.spans + self.place


class QkvWeights(Extra):
    n_in, n_out = 2, 2
    met = True

    def __init__(self, spans, chips, cut, ids):
        self.spans, self.chips = spans, chips
        self.members, self.block, self.columns = cut.shape
        self.ids_shape = ids.shape
        vmem = pl.BlockSpec(memory_space=pltpu.VMEM)
        self.out_shapes = [
            jax.ShapeDtypeStruct((chips * self.members * self.block, self.columns), BF16),
            jax.ShapeDtypeStruct((self.members * ids.shape[0], ids.shape[1]), jnp.int32),
        ]
        self.out_specs = [vmem, vmem]

    def scratch(self):
        rows = self.chips * self.members * self.block
        sems = pltpu.SemaphoreType.DMA((self.members,))
        cross = pltpu.SemaphoreType.DMA((self.chips, self.members))
        ids = (self.members * self.ids_shape[0], self.ids_shape[1])
        return [pltpu.VMEM((rows, self.columns), BF16), pltpu.VMEM(ids, jnp.int32)] + [sems] * 4 + [cross] * 2

    def at(self, chip, m):
        return pl.ds(pl.multiple_of((chip * self.members + m) * self.block, self.block), self.block)

    def ids_at(self, m):
        return pl.ds(pl.multiple_of(m * self.ids_shape[0], self.ids_shape[0]), self.ids_shape[0])

    def block_copy(self, s):
        full, _, send, recv = self.held[:4]
        core, place = step_member(self.core, self.place, s, self.spans)
        return self.remote(
            self.ins[0].at[core * self.spans + place], full.at[self.at(self.chip, self.me)],
            send.at[s], recv.at[s], core=core, ctx=place,
        )

    def ids_copy(self, s):
        all_ids, send, recv = self.held[1], self.held[4], self.held[5]
        core, place = step_member(self.core, self.place, s, self.spans)
        return self.remote(
            self.ins[1], all_ids.at[self.ids_at(self.me)], send.at[s], recv.at[s], core=core, ctx=place
        )

    def source(self, s):
        core = lax.rem(self.core + s % 2, 2)
        return core * self.spans + lax.rem(self.place + self.spans - s // 2, self.spans)

    def chip_copy(self, s, m):
        full, _, _, _, _, _, send, recv = self.held
        where = self.at(self.chip, m)
        return self.remote(
            full.at[where], full.at[where], send.at[s, m], recv.at[s, m], chip=lax.rem(self.chip + s, self.chips)
        )

    def square_copy(self, kind, s):
        full, _, _, _, _, _, send, recv = self.held
        along_x, along_y, _ = square(self.chip)
        m = self.me if s == 0 else self.source(s)
        owner = self.chip if kind < 2 else (along_x if s % 2 == 0 else along_y)
        to = (along_x, along_y, along_y if s % 2 == 0 else along_x)[kind]
        where = self.at(owner, m)
        return self.remote(full.at[where], full.at[where], send.at[kind, s], recv.at[kind, s], chip=to)

    def start(self):
        self.locate()
        cut, ids = self.ins
        full, all_ids = self.held[:2]
        for s in range(1, self.members):
            self.block_copy(s).start()
        for s in range(1, self.members):
            self.ids_copy(s).start()
        full[self.at(self.chip, self.me), :] = cut[self.me]
        all_ids[self.ids_at(self.me), :] = ids[...]

    def send_block(self, s):
        m = self.me if s == 0 else self.source(s)
        if s > 0:
            self.block_copy(s).wait_recv()
        if self.chips == 4:
            for kind in (0, 1) if s % 2 == 0 else (1, 0):
                self.square_copy(kind, s).start()
            return
        for step in range(1, self.chips):
            self.chip_copy(step, m).start()

    def pass_block(self, s):
        self.square_copy(s % 2, s).wait_recv()
        self.square_copy(2, s).start()

    def tick(self, t):
        @pl.when(t == 0)
        def _():
            for s in range(self.members):
                self.send_block(s)

        half = self.members // 2
        for n in range(2):

            @pl.when(t == PASS_AT + n)
            def _():
                if self.chips == 4:
                    for s in range(n * half, (n + 1) * half):
                        self.pass_block(s)
                if n == 1:
                    self.after_blocks()

    def finish(self, ticks):
        full, all_ids = self.held[:2]
        for s in range(1, self.members):
            self.ids_copy(s).wait_recv()
            self.block_copy(s).wait_send()
            self.ids_copy(s).wait_send()

        if self.chips == 4:
            for s in range(self.members):
                for kind in range(3):
                    self.square_copy(kind, s).wait_send()
                    if kind != s % 2:
                        self.square_copy(kind, s).wait_recv()
        else:

            @pl.loop(0, self.members)
            def _(m):
                for s in range(1, self.chips):
                    self.chip_copy(s, m).wait()

        self.outs[0][...] = full[...]
        self.outs[1][...] = all_ids[...]


class QkvGrads(Extra):
    n_in, n_out = 3, 3
    met = True

    def __init__(self, spans, chips, members, grads, sums, out_grads):
        self.spans, self.chips, self.members = spans, chips, members
        self.out_rows = out_grads.shape[0] // chips
        self.block, self.columns = grads.shape[0] // (chips * members), grads.shape[1]
        self.part = self.columns // 3
        self.width = self.part * members
        self.own_rows = self.part // 128
        self.sum_rows = sums.shape[0]
        vmem = pl.BlockSpec(memory_space=pltpu.VMEM)
        self.out_shapes = [
            jax.ShapeDtypeStruct((self.block, 3 * self.width), F32),
            jax.ShapeDtypeStruct((4, self.width // 128, 128), F32),
            jax.ShapeDtypeStruct((self.out_rows, self.width), F32),
        ]
        self.out_specs = [vmem] * 3

    def scratch(self):
        sems = pltpu.SemaphoreType.DMA((self.members,))
        chip_sems = pltpu.SemaphoreType.DMA((self.chips,))
        cross = pltpu.SemaphoreType.DMA((self.chips, self.members))
        return [
            pltpu.VMEM((self.chips, self.members, self.block, self.columns), BF16),
            pltpu.VMEM((self.members, self.block, self.columns), BF16),
            pltpu.VMEM((self.members, self.block, self.columns), BF16),
            pltpu.VMEM((self.members, self.block, self.columns), BF16),
            pltpu.VMEM((self.chips, self.sum_rows, 128), F32),
            pltpu.VMEM((self.sum_rows, 128), F32),
            pltpu.VMEM((self.members, self.sum_rows, 128), F32),
            pltpu.VMEM((self.chips, self.out_rows, self.width), BF16),
            pltpu.VMEM((self.out_rows, self.width), BF16),
            pltpu.VMEM((self.out_rows, self.width), BF16),
        ] + [cross] * 2 + [sems] * 2 + [chip_sems] * 2 + [sems] * 2 + [chip_sems] * 2 + [pltpu.SemaphoreType.DMA] * 2

    def at(self, chip, m):
        return pl.ds(pl.multiple_of((chip * self.members + m) * self.block, self.block), self.block)

    def chip_copy(self, s, m):
        other = lax.rem(self.chip + s, self.chips)
        return self.remote(
            self.ins[0].at[self.at(other, m)], self.arrived.at[s, m],
            self.cross_send.at[s, m], self.cross_recv.at[s, m], chip=other,
        )

    def member_copy(self, s):
        core, place = step_member(self.core, self.place, s, self.spans)
        return self.remote(
            self.summed.at[core * self.spans + place], self.columns_in.at[self.me],
            self.member_send.at[s], self.member_recv.at[s], core=core, ctx=place,
        )

    def sums_chip(self, s):
        return self.remote(
            self.ins[1], self.sums_in.at[s], self.sums_send.at[s], self.sums_recv.at[s],
            chip=lax.rem(self.chip + s, self.chips),
        )

    def sums_member(self, s):
        core, place = step_member(self.core, self.place, s, self.spans)
        return self.remote(
            self.sums_chips, self.sums_members.at[self.me], self.last_send.at[s], self.last_recv.at[s],
            core=core, ctx=place,
        )

    def out_copy(self, s):
        other = lax.rem(self.chip + s, self.chips)
        rows = pl.ds(pl.multiple_of(other * self.out_rows, self.out_rows), self.out_rows)
        return self.remote(
            self.ins[2].at[rows], self.out_in.at[s], self.out_send.at[s], self.out_recv.at[s], chip=other
        )

    def move_copy(self):
        chip, core, place = owner_of(self.chip, self.core, self.place, self.spans)
        return self.remote(
            self.out_sum, self.out_final, self.move_send, self.move_recv, chip=chip, core=core, ctx=place
        )

    def square_copy(self, kind, i):
        along_x, along_y, across = square(self.chip)
        m = self.nth(i)
        first, second = (along_x, along_y) if i % 2 == 0 else (along_y, along_x)
        if kind == 2:
            src, to = self.passing.at[m], second
        else:
            src, to = self.ins[0].at[self.at((across, first)[kind], m)], first
        return self.remote(
            src, self.arrived.at[kind, m], self.cross_send.at[kind, m], self.cross_recv.at[kind, m], chip=to
        )

    def nth(self, i):
        return lax.rem(self.me + 1 + i, self.members)

    def pass_blocks(self):
        along_x, along_y, _ = square(self.chip)
        for i in range(self.members):
            m = self.nth(i)
            self.square_copy(0, i).wait_recv()
            mine = self.ins[0][self.at(along_y if i % 2 == 0 else along_x, m), :]
            self.passing[m] = (mine.astype(F32) + self.arrived[0, m].astype(F32)).astype(BF16)
            self.square_copy(2, i).start()

    def begin(self):
        self.locate()
        (
            self.arrived, self.passing, self.summed, self.columns_in, self.sums_in, self.sums_chips, self.sums_members,
            self.out_in, self.out_sum, self.out_final,
            self.cross_send, self.cross_recv, self.member_send, self.member_recv,
            self.sums_send, self.sums_recv, self.last_send, self.last_recv,
            self.out_send, self.out_recv, self.move_send, self.move_recv,
        ) = self.held
        for s in range(1, self.chips):
            self.out_copy(s).start()

    def start(self):
        for s in range(1, self.chips):
            self.sums_chip(s).start()

    def send_shares(self):
        if self.chips == 4:
            for i in range(self.members):
                self.square_copy(0, i).start()
                self.square_copy(1, i).start()
            return

        @pl.loop(0, self.members)
        def _(i):
            m = lax.rem(self.me + 1 + i, self.members)
            for s in range(1, self.chips):
                self.chip_copy(s, m).start()

    def add_block(self, m):
        total = self.ins[0][self.at(self.chip, m), :].astype(F32)
        for s in range(1, 3 if self.chips == 4 else self.chips):
            self.chip_copy(s, m).wait_recv()
            total = total + self.arrived[s, m].astype(F32)
        self.summed[m] = total.astype(BF16)

    def send_blocks(self, first, last):
        for s in range(first, last):
            core, place = step_member(self.core, self.place, s, self.spans)
            self.add_block(core * self.spans + place)
            self.member_copy(s).start()

    def tick(self, t):
        @pl.when(t == 0)
        def _():
            self.work()
            self.send_shares()

        @pl.when(t == LATE_TICK)
        def _():
            self.late()

        if self.chips == 4:

            @pl.when(t == PASS_TICK)
            def _():
                self.pass_blocks()

        @pl.when(t == 1)
        def _():
            total = self.ins[1][...]
            for s in range(1, self.chips):
                self.sums_chip(s).wait_recv()
                total = total + self.sums_in[s]
            self.sums_chips[...] = total
            self.sums_members[self.me] = total
            for s in range(1, self.members):
                self.sums_member(s).start()

        @pl.when(t == 2)
        def _():
            rows = pl.ds(pl.multiple_of(self.chip * self.out_rows, self.out_rows), self.out_rows)
            total = self.ins[2][rows, :].astype(F32)
            for s in range(1, self.chips):
                self.out_copy(s).wait_recv()
                total = total + self.out_in[s].astype(F32)
            self.out_sum[...] = total.astype(BF16)

            @pl.when(stays(self.chip, self.core, self.place, self.spans))
            def _():
                self.out_final[...] = total.astype(BF16)

            @pl.when(jnp.logical_not(stays(self.chip, self.core, self.place, self.spans)))
            def _():
                self.move_copy().start()

    def finish(self, ticks):
        self.send_blocks(1, self.members)
        self.add_block(self.me)
        self.columns_in[self.me] = self.summed[self.me]
        for s in range(1, self.members):
            self.sums_member(s).wait()
        wide = self.width // 128
        for i in range(2):
            total = self.sums_members[0, i * wide : (i + 1) * wide, :]
            for m in range(1, self.members):
                total = total + self.sums_members[m, i * wide : (i + 1) * wide, :]
            self.outs[1][2 + i] = total
            base = 2 * wide + i * self.own_rows
            for m in range(self.members):
                self.outs[1][i, m * self.own_rows : (m + 1) * self.own_rows, :] = self.sums_members[
                    m, base : base + self.own_rows, :
                ]
        for s in range(1, self.members):
            self.member_copy(s).wait()
        for m in range(self.members):
            for i in range(3):
                self.outs[0][:, i * self.width + m * self.part : i * self.width + (m + 1) * self.part] = (
                    self.columns_in[m, :, i * self.part : (i + 1) * self.part].astype(F32)
                )
        @pl.when(jnp.logical_not(stays(self.chip, self.core, self.place, self.spans)))
        def _():
            self.move_copy().wait()

        self.outs[2][...] = self.out_final[...].astype(F32)
        for s in range(1, self.chips):
            self.sums_chip(s).wait_send()
            self.out_copy(s).wait_send()

        @pl.loop(0, self.members)
        def _(m):
            for s in range(3) if self.chips == 4 else range(1, self.chips):
                self.chip_copy(s, m).wait_send()


def rope_tables(positions):
    half = HEAD_DIM // 2
    frequency = ROPE_BASE ** (-(jnp.arange(half, dtype=F32) * 2.0 / HEAD_DIM))
    angles = positions[:, None] * frequency[None, :]
    cosine = jnp.cos(angles)
    sine = jnp.sin(angles)
    return (jnp.concatenate([cosine, cosine], 1), jnp.concatenate([sine, sine], 1))


def dot(left, right):
    return jnp.dot(left, right, preferred_element_type=F32)


def dot_rows(left, right):
    return lax.dot_general(left, right, (((1,), (1,)), ((), ())), preferred_element_type=F32)


def dot_first(left, right):
    return lax.dot_general(left, right, (((0,), (0,)), ((), ())), preferred_element_type=F32)


def gather(values, axes):
    return lax.all_gather(values, axes, axis=0, tiled=True)


def scatter_sum(values, axes):
    return lax.psum_scatter(values, axes, scatter_dimension=0, tiled=True)


FF_TILE = 512
SUM_TILE = 1024
BATCH_PIECE = 16
DOWN_TICK = 6
GRAD_TILE = 256


def square(chip):
    along_x = chip + 1 - 2 * lax.rem(chip, 2)
    return along_x, lax.rem(chip + 2, 4), lax.rem(along_x + 2, 4)


class SquareSum:
    def __init__(self, chip, block, landing, send, recv):
        self.chip, self.block, self.landing, self.send, self.recv = chip, block, landing, send, recv
        self.x, self.y, self.across = square(chip)

    def copy(self, i):
        owner = (self.across, self.across, self.x, self.y, self.y, self.x)[i]
        half = (0, 1, 0, 1, 0, 1)[i]
        to = (self.x, self.y, self.x, self.y, self.y, self.x)[i]
        return pltpu.make_async_remote_copy(
            src_ref=self.block(owner, half), dst_ref=self.landing.at[i], send_sem=self.send.at[i],
            recv_sem=self.recv.at[i], device_id={"chip": to}, device_id_type=MESH_ID,
        )

    def begin(self, first):
        self.copy(first).start()
        self.copy(first + 1).start()

    def relay(self):
        for i, owner, half in ((0, self.y, 0), (1, self.x, 1)):
            self.copy(i).wait_recv()
            ref = self.block(owner, half)
            ref[...] = (ref[...].astype(F32) + self.landing[i].astype(F32)).astype(BF16)
        self.begin(4)

    def finish(self, half):
        for i in (2 + half, 4 + half):
            self.copy(i).wait_recv()
        for i in (0 + half, 2 + half, 4 + half):
            self.copy(i).wait_send()
        total = self.block(self.chip, half)[...].astype(F32)
        return total + self.landing[2 + half].astype(F32) + self.landing[4 + half].astype(F32)


class Middle:
    def __init__(self, spans, rows, width, hidden, piece):
        self.spans, self.rows, self.width, self.hidden, self.piece = spans, rows, width, hidden, piece
        self.count = rows // piece
        self.block = spans * piece
        self.batch = 2 * self.block

    def body(
        self, chips, partial, tokens, cotangent, gains, gate_up, gate_up_w, down,
        output, residual_grad, gain_feed, gain_attn, down_sum, gate_sum, residual_all, feed_grad_all, gate_part, up_part, projected_all,
        residual, projected, own, near, from_left, from_right, held, wide, act, back, up_weights, down_weights, slices, given, landed,
        load_sem, weight_sem, store_sem, slice_sem, part_sem, free_sem, near_send, near_recv, right_send, right_recv, left_send, left_recv,
        fwd_send, fwd_recv, bwd_send, bwd_recv, side_send, side_recv, down_send, down_recv, give_send, give_recv, take_send, take_recv, pass_send, pass_recv,
    ):
        spans, rows, piece, count = self.spans, self.rows, self.piece, self.count
        width, hidden, block, batch = self.width, self.hidden, self.block, self.batch
        core = lax.axis_index("core")
        place = lax.axis_index("ctx")
        other = 1 - core
        last = spans - 1
        has_left = place > 0
        has_right = place < last

        def turn_of(o):
            return jnp.maximum(o, last - o)

        def at(d, k):
            return pl.ds(pl.multiple_of((k * spans + d) * piece, piece), piece)

        def at_seq(seq, d, k):
            return pl.ds(pl.multiple_of(((k * 2 + seq) * spans + d) * piece, piece), piece)

        def batch_at(k):
            return pl.ds(pl.multiple_of(k * batch, batch), batch)

        def natural(seq, d, k):
            return pl.ds(pl.multiple_of((seq * spans + d) * rows + k * piece, piece), piece)

        def remote(src, dst, send, recv, **device):
            return pltpu.make_async_remote_copy(
                src_ref=src, dst_ref=dst, send_sem=send, recv_sem=recv, device_id=device, device_id_type=MESH_ID
            )

        barrier = pltpu.get_barrier_semaphore()
        pl.semaphore_signal(barrier, 1, device_id={"core": other}, device_id_type=MESH_ID)

        @pl.when(has_left)
        def _():
            pl.semaphore_signal(barrier, 1, device_id={"ctx": place - 1}, device_id_type=MESH_ID)

        @pl.when(has_right)
        def _():
            pl.semaphore_signal(barrier, 1, device_id={"ctx": place + 1}, device_id_type=MESH_ID)

        def near_copy(e, d, k):
            src = partial.at[natural(other, d, k)] if e == 0 else own.at[at_seq(other, d, k)]
            return remote(src, near.at[at(d, k)], near_send.at[d, k], near_recv.at[d, k], core=other)

        def right_copy(d, k):
            return remote(
                own.at[at_seq(core, d, k)], from_left.at[at(d, k)], right_send.at[d, k], right_recv.at[d, k],
                ctx=place + 1,
            )

        def left_copy(d, k):
            return remote(
                own.at[at_seq(core, d, k)], from_right.at[at(d, k)], left_send.at[d, k], left_recv.at[d, k],
                ctx=place - 1,
            )

        def spread_copy(o, k, send, recv, **device):
            where = held.at[at_seq(core, o, k)]
            return remote(where, where, send.at[o, k], recv.at[o, k], **device)

        def fwd_copy(o, k):
            return spread_copy(o, k, fwd_send, fwd_recv, ctx=place + 1)

        def bwd_copy(o, k):
            return spread_copy(o, k, bwd_send, bwd_recv, ctx=place - 1)

        def side_copy(o, k):
            return spread_copy(o, k, side_send, side_recv, core=other)

        def load_own(d, k):
            return pltpu.make_async_copy(
                partial.at[natural(core, d, k)], own.at[at_seq(core, d, k)], load_sem.at[d, k]
            )

        @pl.loop(0, count)
        def _(k):
            for d in range(spans):
                load_own(d, k).start()

        chip = lax.axis_index("chip")
        shard = down.shape[0]
        here = pl.ds(pl.multiple_of(chip * shard, shard), shard)
        load_down = pltpu.make_async_copy(down, down_weights.at[here], weight_sem.at[chips])

        if chips == 4:
            along_x, along_y, across = square(chip)

        def load_up(s):
            if s == 0:
                return pltpu.make_async_copy(gate_up, up_weights.at[here], weight_sem.at[0])
            source = (along_x, along_y)[s - 1] if chips == 4 else lax.rem(chip + s, chips)
            there = pl.ds(pl.multiple_of(source * shard, shard), shard)
            return pltpu.make_async_copy(gate_up_w.at[there], up_weights.at[there], weight_sem.at[s])


        loads = 3 if chips == 4 else chips

        def up_copy(i):
            size = shard // 2
            source, to = ((along_x, along_y), (along_y, along_x))[i]
            where = pl.ds(pl.multiple_of(source * shard + i * size, size), size)
            return remote(gate_up_w.at[where], up_weights.at[where], pass_send.at[i], pass_recv.at[i], chip=to)

        def down_copy(s):
            if chips != 4:
                return remote(
                    down, down_weights.at[here], down_send.at[s], down_recv.at[s], chip=lax.rem(chip + s, chips)
                )
            half = (0, 1, 1, 0, 0, 1)[s]
            to = (along_x, along_y, along_x, along_y, along_y, along_x)[s]
            size = shard // 2
            if s < 4:
                src = down.at[half * size : (half + 1) * size]
                at_chip = chip
            else:
                at_chip = (along_x, along_y)[s - 4]
            dst = down_weights.at[pl.ds(pl.multiple_of(at_chip * shard + half * size, size), size)]
            return remote(src if s < 4 else dst, dst, down_send.at[s], down_recv.at[s], chip=to)

        def relay_down():
            for s in range(2):
                down_copy(s).wait_recv()
                down_copy(4 + s).start()

        for s in range(loads):
            load_up(s).start()
        load_down.start()
        gain_feed[...] = jnp.zeros_like(gain_feed)
        gain_attn[...] = jnp.zeros_like(gain_attn)
        for s in range(1, chips):
            pl.semaphore_signal(
                barrier, 1, device_id={"chip": lax.rem(chip + s, chips)}, device_id_type=MESH_ID
            )
        pl.semaphore_wait(barrier, chips + has_left.astype(jnp.int32) + has_right.astype(jnp.int32))
        if chips == 4:
            for i in range(2):
                up_copy(i).start()
        for s in range(4) if chips == 4 else range(1, chips):
            down_copy(s).start()

        @pl.loop(0, count)
        def _(k):
            for d in range(spans):
                near_copy(0, d, k).start()

        def base(e, d, k):
            near_copy(e, d, k).wait_recv()
            if e == 0:
                load_own(d, k).wait()
            return own[at_seq(core, d, k), :].astype(F32) + near[at(d, k), :].astype(F32)

        def pass_on(e, d, k, arrived, copy, later):
            value = base(e, d, k)

            @pl.when(later)
            def _():
                copy(d, k).wait_recv()

            before = arrived[at(d, k), :].astype(F32)
            value = value + jnp.where(later, before, jnp.zeros_like(before))
            own[at_seq(core, d, k), :] = value.astype(BF16)
            copy(d, k).start()

        def pass_right(e, k):
            for d in range(last, 0, -1):

                @pl.when(d > place)
                def _():
                    pass_on(e, d, k, from_left, right_copy, has_left)

        def pass_left(e, k):
            for d in range(last):

                @pl.when(d < place)
                def _():
                    pass_on(e, d, k, from_right, left_copy, has_right)

        def finish(e, k):
            total = base(e, place, k)

            @pl.when(has_left)
            def _():
                right_copy(place, k).wait_recv()

            @pl.when(has_right)
            def _():
                left_copy(place, k).wait_recv()

            zero = jnp.zeros_like(total)
            total = total + jnp.where(has_left, from_left[at(place, k), :].astype(F32), zero)
            total = total + jnp.where(has_right, from_right[at(place, k), :].astype(F32), zero)
            mine = pl.ds(pl.multiple_of(k * piece, piece), piece)
            if e == 0:
                result = after_projected(total, (tokens, gains), (residual, projected), mine)
            elif e == 1:
                result = after_feed(total, (residual, cotangent, gains), (output, gain_feed), mine)
            else:
                result = after_back(total, (projected, cotangent, gains), (residual_grad, gain_attn), mine)
            held[at_seq(core, place, k), :] = result.astype(BF16)

            @pl.when(has_right)
            def _():
                fwd_copy(place, k).start()

            @pl.when(has_left)
            def _():
                bwd_copy(place, k).start()

            side_copy(place, k).start()

        def relay_right(o, k):
            fwd_copy(o, k).wait_recv()

            @pl.when(has_right)
            def _():
                fwd_copy(o, k).start()

            side_copy(o, k).start()

        def relay_left(o, k):
            bwd_copy(o, k).wait_recv()

            @pl.when(has_left)
            def _():
                bwd_copy(o, k).start()

            side_copy(o, k).start()

        def gathered(k):
            for o in range(spans):
                side_copy(o, k).wait_recv()

        def sums_sent(e, k):
            for d in range(spans):
                near_copy(e, d, k).wait_send()

                @pl.when(d > place)
                def _():
                    right_copy(d, k).wait_send()

                @pl.when(d < place)
                def _():
                    left_copy(d, k).wait_send()

        def spread_sent(k):
            for o in range(spans):
                side_copy(o, k).wait_send()

                @pl.when(jnp.logical_and(o <= place, has_right))
                def _():
                    fwd_copy(o, k).wait_send()

                @pl.when(jnp.logical_and(o >= place, has_left))
                def _():
                    bwd_copy(o, k).wait_send()

        def store(src, dst, k, sem):
            return pltpu.make_async_copy(src, dst.at[batch_at(k)], sem)

        def forward(k):
            @pl.when(k == 0)
            def _():
                for s in range(loads):
                    load_up(s).wait()
                if chips == 4:
                    for i in range(2):
                        up_copy(i).wait()

            gathered(k)
            keep = store(held.at[batch_at(k)], residual_all, k, store_sem.at[0])
            keep.start()

            @pl.loop(0, hidden // FF_TILE)
            def _(n):
                low = pl.ds(pl.multiple_of(n * FF_TILE, FF_TILE), FF_TILE)
                high = pl.ds(pl.multiple_of(hidden + n * FF_TILE, FF_TILE), FF_TILE)
                gate = dot(held[batch_at(k), :], up_weights[:, low])
                up = dot(held[batch_at(k), :], up_weights[:, high])
                wide[batch_at(k), low] = gate
                wide[batch_at(k), high] = up
                act[batch_at(k), low] = (gate * (1.0 / (1.0 + jnp.exp(-gate))) * up).astype(BF16)

            sums_sent(0, k)

            @pl.when(k == 0)
            def _():
                load_down.wait()
                for s in range(1, chips) if chips != 4 else range(6):
                    down_copy(s).wait_send()
                    if chips != 4 or s >= 2:
                        down_copy(s).wait_recv()

            @pl.loop(0, width // SUM_TILE)
            def _(n):
                columns = pl.ds(pl.multiple_of(n * SUM_TILE, SUM_TILE), SUM_TILE)
                own[batch_at(k), columns] = dot_rows(act[batch_at(k), :], down_weights[columns, :]).astype(BF16)

            keep.wait()
            spread_sent(k)
            for d in range(spans):
                near_copy(1, d, k).start()

        down_tiles = width // GRAD_TILE
        per_chip = shard // GRAD_TILE

        def tile_rows(n):
            return pl.ds(pl.multiple_of(n * GRAD_TILE, GRAD_TILE), GRAD_TILE)

        if chips == 4:
            assert per_chip == 2
            turns = [(across, 0), (across, 1), (along_x, 0), (along_y, 1), (along_y, 0), (along_x, 1), (chip, 0), (chip, 1)]
            order = [owner * per_chip + half for owner, half in turns]
        else:
            order = [lax.rem(chip + 1 + j // per_chip, chips) * per_chip + j % per_chip for j in range(down_tiles)]
        tiles = [(m, order[j] if m < 2 else j) for m in range(3) for j in range(down_tiles)]

        def load_slice(j):
            m, n = tiles[j]
            source = feed_grad_all if m == 0 else residual_all
            return pltpu.make_async_copy(source.at[:, tile_rows(n)], slices.at[j % 4], slice_sem.at[j % 4])

        def half_at(owner, half):
            return pl.ds(pl.multiple_of((owner * per_chip + half) * GRAD_TILE, GRAD_TILE), GRAD_TILE)

        if chips == 4:
            sums = [
                SquareSum(
                    chip, lambda owner, half: given.at[half_at(owner, half)], landed.at[0], give_send, give_recv
                ),
                SquareSum(
                    chip, lambda owner, half: up_weights.at[half_at(owner, half), :hidden], landed.at[1], take_send, take_recv
                ),
            ]

        def give_copy(s):
            theirs = pl.ds(pl.multiple_of(lax.rem(chip + s, chips) * shard, shard), shard)
            return remote(
                given.at[theirs], down_weights.at[s * shard : (s + 1) * shard], give_send.at[s], give_recv.at[s],
                chip=lax.rem(chip + s, chips),
            )

        def part_copy(n, m):
            half = slice((m - 1) * hidden, m * hidden)
            return pltpu.make_async_copy(
                up_weights.at[tile_rows(n), half], (gate_part, up_part)[m - 1].at[tile_rows(n)], part_sem.at[m - 1, n]
            )

        def work_out(j):
            if j + 2 < len(tiles):
                load_slice(j + 2).start()
            load_slice(j).wait()
            m, n = tiles[j]
            if m == 0:
                given[tile_rows(n), :] = dot_first(slices[j % 4], act[...]).astype(BF16)
            else:
                half = slice((m - 1) * hidden, m * hidden)
                up_weights[tile_rows(n), half] = dot_first(slices[j % 4], back[:, half]).astype(BF16)

        def weight_grads(q):
            if chips == 4:
                m, r = q // 4, q % 4
                if m < 2:
                    for j in range(m * down_tiles + 2 * r, m * down_tiles + 2 * r + 2):
                        work_out(j)
                    if r < 2:
                        sums[m].begin(2 * r)
                    elif r == 2:
                        sums[m].relay()
                else:
                    for j in range(2 * down_tiles, 3 * down_tiles):
                        work_out(j)
                        part_copy(tiles[j][1], 2).start()
                return
            if q < chips:
                for j in range(q * per_chip, (q + 1) * per_chip):
                    work_out(j)
                if q == 0:
                    pl.semaphore_wait(free_sem, chips - 1)
                if q < chips - 1:
                    give_copy(q + 1).start()
                return
            first = down_tiles + 4 * (q - chips)
            for j in range(first, min(first + 4, len(tiles))):
                work_out(j)
                part_copy(tiles[j][1], tiles[j][0]).start()

        def backward(k):
            gathered(k)
            keep = store(held.at[batch_at(k)], feed_grad_all, k, store_sem.at[0])
            keep.start()

            @pl.loop(0, hidden // FF_TILE)
            def _(n):
                low = pl.ds(pl.multiple_of(n * FF_TILE, FF_TILE), FF_TILE)
                high = pl.ds(pl.multiple_of(hidden + n * FF_TILE, FF_TILE), FF_TILE)
                act_grad = dot(held[batch_at(k), :], down_weights[:, low])
                gate = wide[batch_at(k), low]
                up = wide[batch_at(k), high]
                sigmoid = 1.0 / (1.0 + jnp.exp(-gate))
                back[batch_at(k), low] = (act_grad * up * sigmoid * (1.0 + gate * (1.0 - sigmoid))).astype(BF16)
                back[batch_at(k), high] = (act_grad * (gate * sigmoid)).astype(BF16)

            sums_sent(1, k)

            @pl.loop(0, width // SUM_TILE)
            def _(n):
                columns = pl.ds(pl.multiple_of(n * SUM_TILE, SUM_TILE), SUM_TILE)
                own[batch_at(k), columns] = dot_rows(back[batch_at(k), :], up_weights[columns, :]).astype(BF16)

            keep.wait()
            spread_sent(k)
            for d in range(spans):
                near_copy(2, d, k).start()

            @pl.when(k == count - 1)
            def _():
                for s in range(1, chips) if chips != 4 else ():
                    pl.semaphore_signal(
                        free_sem, 1, device_id={"chip": lax.rem(chip + s, chips)}, device_id_type=MESH_ID
                    )
                load_slice(0).start()
                load_slice(1).start()

        def give(seq, d, k):
            return pltpu.make_async_copy(
                held.at[at_seq(seq, d, k)], projected_all.at[natural(seq, d, k)], load_sem.at[d, k]
            )

        def hand_out(k):
            gathered(k)
            sums_sent(2, k)
            for seq in range(2):
                for d in range(spans):
                    give(seq, d, k).start()
                for d in range(spans):
                    give(seq, d, k).wait()
            spread_sent(k)

        step = 2 * last + 2
        last_steps = 9 if chips == 4 else chips + down_tiles // 2
        assert last_steps <= step + 1

        def due(t, run):
            @pl.when(jnp.logical_and(t >= 0, t < count))
            def _():
                run(t)

        @pl.loop(0, 3 * step + count - 1)
        def _(t):
            for e in range(2, -1, -1):
                now = t - e * step
                for j in range(1, spans):
                    o = place - j

                    @pl.when(o >= 0)
                    def _():
                        due(now - turn_of(o) - j, functools.partial(relay_right, o))

                    p = place + j

                    @pl.when(p < spans)
                    def _():
                        due(now - turn_of(p) - j, functools.partial(relay_left, p))

                due(now - place, functools.partial(pass_right, e))
                due(now - (last - place), functools.partial(pass_left, e))
                due(now - turn_of(place), functools.partial(finish, e))
            if chips == 4:

                @pl.when(t == DOWN_TICK)
                def _():
                    relay_down()

            for e, run in ((2, hand_out), (1, backward), (0, forward)):
                due(t - e * step - 2 * last, run)
            for q in range(last_steps):

                @pl.when(t == count + step + 2 * last + q)
                def _():
                    weight_grads(q)

        if chips == 4:
            for group, out in zip(sums, (down_sum, gate_sum)):
                for half in range(2):
                    out[half * GRAD_TILE : (half + 1) * GRAD_TILE, :] = group.finish(half).astype(BF16)
            for n in range(down_tiles):
                part_copy(n, 2).wait()
            return
        total = given[here, :].astype(F32)
        for s in range(1, chips):
            give_copy(s).wait()
            total = total + down_weights[s * shard : (s + 1) * shard, :].astype(F32)
        down_sum[...] = total.astype(BF16)
        gate_sum[...] = jnp.zeros_like(gate_sum)
        for n in range(down_tiles):
            part_copy(n, 1).wait()
            part_copy(n, 2).wait()

    def call(self, chips, partial, tokens, cotangent, gains, gate_up, gate_up_w, down):
        spans, rows, width, hidden, count = self.spans, self.rows, self.width, self.hidden, self.count
        total = 2 * spans * rows
        vmem = pl.BlockSpec(memory_space=pltpu.VMEM)
        hbm = pl.BlockSpec(memory_space=pl.ANY)
        shape = jax.ShapeDtypeStruct
        sems = pltpu.SemaphoreType.DMA((spans, count))
        two = pltpu.SemaphoreType.DMA((2,))
        return pl.pallas_call(
            functools.partial(self.body, chips),
            out_shape=[
                shape((rows, width), BF16),
                shape((rows, width), F32),
                shape((1, width), F32),
                shape((1, width), F32),
                shape(down.shape, BF16),
                shape(down.shape, BF16),
                shape((total, width), BF16),
                shape((total, width), BF16),
                shape((16, 128) if chips == 4 else (width, hidden), BF16),
                shape((width, hidden), BF16),
                shape((total, width), BF16),
            ],
            in_specs=[hbm, vmem, vmem, vmem, hbm, hbm, hbm],
            out_specs=[vmem] * 6 + [hbm] * 5,
            scratch_shapes=[
                pltpu.VMEM((rows, width), F32),
                pltpu.VMEM((rows, width), F32),
                pltpu.VMEM((total, width), BF16),
                pltpu.VMEM((total // 2, width), BF16),
                pltpu.VMEM((total // 2, width), BF16),
                pltpu.VMEM((total // 2, width), BF16),
                pltpu.VMEM((total, width), BF16),
                pltpu.VMEM((total, 2 * hidden), F32),
                pltpu.VMEM((total, hidden), BF16),
                pltpu.VMEM((total, 2 * hidden), BF16),
                pltpu.VMEM((width, 2 * hidden), BF16),
                pltpu.VMEM((width, hidden), BF16),
                pltpu.VMEM((4, total, GRAD_TILE), BF16),
                pltpu.VMEM((width, hidden), BF16),
                pltpu.VMEM((2, 6, GRAD_TILE, hidden) if chips == 4 else (2, 6, 16, 128), BF16),
                sems,
                pltpu.SemaphoreType.DMA((chips + 1,)),
                two,
                pltpu.SemaphoreType.DMA((4,)),
                pltpu.SemaphoreType.DMA((2, width // GRAD_TILE)),
                pltpu.SemaphoreType.REGULAR,
            ]
            + [sems] * 12
            + [pltpu.SemaphoreType.DMA((max(chips, 6),))] * 8,
            compiler_params=pltpu.CompilerParams(
                collective_id=2, has_side_effects=True, vmem_limit_bytes=62 << 20
            ),
            cost_estimate=pl.CostEstimate(
                flops=36 * rows * spans * width * hidden, bytes_accessed=100 * width * width, transcendentals=0
            ),
            name="feed_forward",
        )(partial, tokens, cotangent, gains, gate_up, gate_up_w, down)


def turn(values, cosine, sine):
    return values * cosine + pltpu.roll(values, HEAD_DIM // 2, 1) * sine


def row_sums(values):
    total = values[:, :128]
    for first in range(128, values.shape[1], 128):
        total = total + values[:, first : first + 128]
    return jnp.sum(jnp.transpose(total), axis=0, keepdims=True)


def down_rows(row):
    return jnp.transpose(jnp.broadcast_to(row, (128, row.shape[1])))


class Stats:
    def __init__(self, spans, own, arrived, send, recv):
        self.spans, self.own, self.arrived, self.send, self.recv = spans, own, arrived, send, recv
        self.core, self.place = lax.axis_index("core"), lax.axis_index("ctx")
        self.me = self.core * spans + self.place

    def member(self, s):
        core, place = step_member(self.core, self.place, s, self.spans)
        return {"core": core, "ctx": place}

    def greet(self):
        for s in range(1, 2 * self.spans):
            pl.semaphore_signal(
                pltpu.get_barrier_semaphore(), 1, device_id=self.member(s), device_id_type=MESH_ID
            )

    def meet(self):
        pl.semaphore_wait(pltpu.get_barrier_semaphore(), 2 * self.spans - 1)

    def copy(self, s):
        return pltpu.make_async_remote_copy(
            src_ref=self.own, dst_ref=self.arrived.at[s], send_sem=self.send.at[s], recv_sem=self.recv.at[s],
            device_id=self.member(s), device_id_type=MESH_ID,
        )

    def start(self):
        for s in range(1, 2 * self.spans):
            self.copy(s).start()

    def total(self):
        total = self.own[...]
        for s in range(1, 2 * self.spans):
            self.copy(s).wait()
            total = total + self.arrived[s]
        return total


def stats_scratch(spans, total_rows):
    sems = pltpu.SemaphoreType.DMA((2 * spans,))
    return [
        pltpu.VMEM((8, total_rows), F32),
        pltpu.VMEM((2 * spans, 8, total_rows), F32),
        sems,
        sems,
    ]


def allowed_at(ids, seq, block, count, spans):
    rows = ids.shape[1]
    per = block // rows
    ids_of = lambda z: ids[(seq * spans + z) * 8 : (seq * spans + z) * 8 + 8, :].astype(F32)
    first = count * per
    keys = jnp.concatenate([ids_of(z)[:1] for z in range(first + per)], 1)
    queries = jnp.concatenate([jnp.transpose(ids_of(z))[:, :1] for z in range(first, first + per)], 0)
    shape = (block, (count + 1) * block)
    query_at = lax.broadcasted_iota(jnp.int32, shape, 0) + count * block
    key_at = lax.broadcasted_iota(jnp.int32, shape, 1)
    same = queries == keys
    seen = jnp.logical_and(same, key_at <= query_at)
    return jnp.logical_and(seen, jnp.logical_or(keys != 0.0, key_at == query_at))


def softmax_parts(query, key, allowed):
    scores = jnp.where(allowed, dot_rows(query, key) * HEAD_DIM ** (-0.5), -1e30)
    weights = jnp.exp(scores - jnp.max(scores, axis=1, keepdims=True))
    return weights / jnp.sum(weights, axis=1, keepdims=True)


QUERY_BLOCK = 256
ROW_TILE = 256


class Neighbours:
    pieces = 4

    def __init__(self, chip, shard, full, send, recv):
        self.chip, self.shard, self.full, self.send, self.recv = chip, shard, full, send, recv
        self.to = square(chip)[:2]

    def copy(self, i, n):
        size = self.shard.shape[0] // self.pieces
        where = self.full.at[pl.ds(pl.multiple_of(self.chip * self.shard.shape[0] + n * size, size), size)]
        return pltpu.make_async_remote_copy(
            src_ref=self.shard.at[n * size : (n + 1) * size], dst_ref=where,
            send_sem=self.send.at[i, n], recv_sem=self.recv.at[i, n],
            device_id={"chip": self.to[i]}, device_id_type=MESH_ID,
        )

    def begin(self):
        for n in range(self.pieces):
            for i in range(2):
                self.copy(i, n).start()

    def finish(self):
        for n in range(self.pieces):
            for i in range(2):
                self.copy(i, n).wait()


def attend_body(
    spans, chips, exchange, extra, n_scratch,
    tokens, cut, own_ids, w_out, gate_up, gains, cosine, sine,
    weights_out, ids, tokens_all, gate_up_w,
    partial_out, out_w_out, query_out, key_out, value_out, normed_out, factor_out, attended_out,
    raw, given, out_w, moved, own, arrived, store_sem, chip_send, chip_recv, send, recv, move_send, move_recv,
    up_send, up_recv, *rest,
):
    part = out_w.shape[0]
    total_rows = raw.shape[0]
    length = total_rows // 2
    width = tokens.shape[1]
    tiles = total_rows // ROW_TILE
    held, held_w = rest[0], rest[n_scratch]
    stats = Stats(spans, own, arrived, send, recv)
    greet_all(spans, True)
    chip, core, place = lax.axis_index("chip"), stats.core, stats.place
    shard = moved.shape[0]
    here = pl.ds(pl.multiple_of(chip * shard, shard), shard)

    def at(i):
        return pl.ds(pl.multiple_of(i * ROW_TILE, ROW_TILE), ROW_TILE)

    def chip_copy(s):
        return pltpu.make_async_remote_copy(
            src_ref=moved, dst_ref=out_w.at[here], send_sem=chip_send.at[s], recv_sem=chip_recv.at[s],
            device_id={"chip": lax.rem(chip + s, chips)}, device_id_type=MESH_ID,
        )

    def move_copy():
        to_chip, to_core, to_place = summer_of(chip, core, place, spans)
        return pltpu.make_async_remote_copy(
            src_ref=w_out, dst_ref=moved, send_sem=move_send, recv_sem=move_recv,
            device_id={"chip": to_chip, "core": to_core, "ctx": to_place}, device_id_type=MESH_ID,
        )

    home = stays(chip, core, place, spans)
    if chips == 4:
        up = Neighbours(chip, gate_up, gate_up_w, up_send, up_recv)
    own[...] = jnp.zeros_like(own)
    wait_all(spans, True)

    @pl.when(home)
    def _():
        moved[...] = w_out[...]

    @pl.when(jnp.logical_not(home))
    def _():
        move_copy().start()

    def after_blocks():
        @pl.when(jnp.logical_not(home))
        def _():
            move_copy().wait()

        for s in range(1, chips):
            chip_copy(s).start()
        out_w[here, :] = moved[...]
        if chips == 4:
            up.begin()

    extra.after_blocks = after_blocks
    exchange.body(tokens, cut, own_ids, weights_out, ids, tokens_all, *rest)

    @pl.loop(0, tiles)
    def _(i):
        values = dot(held[at(i), :], held_w[...])
        raw[at(i), :] = values
        for n in range(2):
            some = values[:, n * part : (n + 1) * part]
            own[n : n + 1, at(i)] = row_sums(some * some)

    stats.start()

    @pl.loop(0, tiles)
    def _(i):
        value_out[at(i), :] = raw[at(i), 2 * part :].astype(BF16)

    factor_out[...] = lax.rsqrt(stats.total() / width + EPS)
    me = stats.me
    columns = pl.ds(pl.multiple_of(me * part, part), part)
    gain = jnp.concatenate([gains[0:1, columns], gains[1:2, columns]], 1)

    @pl.loop(0, tiles)
    def _(i):
        by_query, by_key = down_rows(factor_out[0:1, at(i)]), down_rows(factor_out[1:2, at(i)])
        place = pl.ds(pl.multiple_of(lax.rem(i, length // ROW_TILE) * ROW_TILE, ROW_TILE), ROW_TILE)
        for h in range(part // HEAD_DIM):
            head = slice(h * HEAD_DIM, (h + 1) * HEAD_DIM)
            low = slice(part + h * HEAD_DIM, part + (h + 1) * HEAD_DIM)
            for out, by, where in ((query_out, by_query, head), (key_out, by_key, low)):
                normed = raw[at(i), where] * by
                normed_out[at(i), where] = normed
                out[at(i), head] = turn(normed * gain[:, where], cosine[place, :], sine[place, :]).astype(BF16)

    for s in range(1, chips):
        chip_copy(s).wait()
    out_w_out[...] = out_w[...]
    block = QUERY_BLOCK
    for seq in range(2):
        for count in range(length // block):
            allowed = allowed_at(ids, seq, block, count, spans)
            rows = slice(seq * length + count * block, seq * length + (count + 1) * block)
            keys = slice(seq * length, seq * length + (count + 1) * block)
            for h in range(part // HEAD_DIM):
                head = slice(h * HEAD_DIM, (h + 1) * HEAD_DIM)
                shares = softmax_parts(query_out[rows, head], key_out[keys, head], allowed)
                attended_out[rows, head] = dot(shares.astype(BF16), value_out[keys, head]).astype(BF16)
            i = rows.start // ROW_TILE
            if i >= 2:
                pltpu.make_async_copy(given.at[i % 2], partial_out.at[at(i - 2)], store_sem.at[i - 2]).wait()
            given[i % 2] = dot(attended_out[rows, :], out_w[...]).astype(BF16)
            pltpu.make_async_copy(given.at[i % 2], partial_out.at[at(i)], store_sem.at[i]).start()
    for i in range(tiles - 2, tiles):
        pltpu.make_async_copy(given.at[i % 2], partial_out.at[at(i)], store_sem.at[i]).wait()
    if chips == 4:
        up.finish()


def attend(spans, chips, tokens, cut, ids, w_out, gate_up, gains, cosine, sine):
    rows, width = tokens.shape
    total_rows = 2 * spans * rows
    part = w_out.shape[0] * chips
    tiles = total_rows // ROW_TILE
    vmem = pl.BlockSpec(memory_space=pltpu.VMEM)
    hbm = pl.BlockSpec(memory_space=pl.ANY)
    shape = jax.ShapeDtypeStruct
    extra = QkvWeights(spans, chips, cut, ids)
    exchange = Exchange(spans, rows, width, PIECE, False, True, pass_tokens, 1, 0, None, extra)
    scratch = exchange.scratch()
    return pl.pallas_call(
        functools.partial(attend_body, spans, chips, exchange, extra, len(scratch) - len(extra.scratch())),
        out_shape=[
            *extra.out_shapes,
            shape((total_rows, width), BF16),
            shape((chips * gate_up.shape[0] if chips == 4 else 16, gate_up.shape[1]), BF16),
            shape((total_rows, width), BF16),
            shape((part, width), BF16),
            shape((total_rows, part), BF16),
            shape((total_rows, part), BF16),
            shape((total_rows, part), BF16),
            shape((total_rows, 2 * part), F32),
            shape((8, total_rows), F32),
            shape((total_rows, part), BF16),
        ],
        in_specs=[vmem] * 4 + [hbm] + [vmem] * 3,
        out_specs=[vmem] * 2 + [hbm] * 3 + [vmem] * 7,
        scratch_shapes=[
            pltpu.VMEM((total_rows, 3 * part), F32),
            pltpu.VMEM((2, ROW_TILE, width), BF16),
            pltpu.VMEM((part, width), BF16),
            pltpu.VMEM(w_out.shape, BF16),
            *stats_scratch(spans, total_rows)[:2],
            pltpu.SemaphoreType.DMA((tiles,)),
            pltpu.SemaphoreType.DMA((chips,)),
            pltpu.SemaphoreType.DMA((chips,)),
            *stats_scratch(spans, total_rows)[2:],
            pltpu.SemaphoreType.DMA,
            pltpu.SemaphoreType.DMA,
            pltpu.SemaphoreType.DMA((2, Neighbours.pieces)),
            pltpu.SemaphoreType.DMA((2, Neighbours.pieces)),
            *scratch,
        ],
        compiler_params=pltpu.CompilerParams(collective_id=1, has_side_effects=True, vmem_limit_bytes=58 << 20),
        cost_estimate=pl.CostEstimate(
            flops=2 * total_rows * width * 5 * part, bytes_accessed=50 * width * width, transcendentals=0
        ),
        name="attend",
    )(tokens, cut, ids, w_out, gate_up, gains, cosine, sine)


def attend_back_body(
    spans, chips, exchange, extra, n_scratch,
    grads, tokens, weights, up_part, out_w, gains, ids, cosine, sine, residual_grad, gain_attn, gain_feed,
    query, key, value, normed, factor, attended,
    input_grad, grad_qkv, grad_gains, grad_out, up_sum,
    held, held_tokens, held_w, raw, mixed, attended_grad, own, arrived, load_sem, send, recv,
    qkv_part, out_part, sums, up_held, up_landed, up_send, up_recv, *rest,
):
    part = out_w.shape[0]
    total_rows = raw.shape[0]
    length = total_rows // 2
    width = grads.shape[1]
    tiles = total_rows // ROW_TILE
    scale = HEAD_DIM ** (-0.5)
    stats = Stats(spans, own, arrived, send, recv)
    greet_all(spans, True)

    def at(i):
        return pl.ds(pl.multiple_of(i * ROW_TILE, ROW_TILE), ROW_TILE)

    def load_rows(i):
        return pltpu.make_async_copy(grads.at[at(i)], held.at[at(i)], load_sem.at[i])

    @pl.loop(0, tiles)
    def _(i):
        load_rows(i).start()

    own[...] = jnp.zeros_like(own)
    load_w = pltpu.make_async_copy(weights, held_w, load_sem.at[tiles])
    load_tokens = pltpu.make_async_copy(tokens, held_tokens, load_sem.at[tiles + 1])
    load_w.start()
    load_tokens.start()
    if chips == 4:
        load_up = pltpu.make_async_copy(up_part, up_held, load_sem.at[tiles + 2])
        load_up.start()
    me = stats.me
    columns = pl.ds(pl.multiple_of(me * part, part), part)
    gain = jnp.concatenate([gains[0:1, columns], gains[1:2, columns]], 1)

    @pl.loop(0, tiles)
    def _(i):
        load_rows(i).wait()
        attended_grad[at(i), :] = dot_rows(held[at(i), :], out_w[...]).astype(BF16)

    out_part[...] = dot_first(attended[...], held[...]).astype(BF16)
    wait_all(spans, True)
    extra.ins = [qkv_part, sums, out_part]
    extra.held = list(rest[n_scratch:])
    extra.begin()
    if chips == 4:
        load_up.wait()
        half_rows = width // 8
        up_sums = SquareSum(
            lax.axis_index("chip"),
            lambda owner, half: up_held.at[
                pl.ds(pl.multiple_of((owner * 2 + half) * half_rows, half_rows), half_rows)
            ],
            up_landed, up_send, up_recv,
        )
        up_sums.begin(0)
        up_sums.begin(2)
    block = QUERY_BLOCK
    blocks = length // block
    for seq in range(2):
        for h in range(part // HEAD_DIM):
            head = slice(h * HEAD_DIM, (h + 1) * HEAD_DIM)
            key_at = slice(part + h * HEAD_DIM, part + (h + 1) * HEAD_DIM)
            value_at = slice(2 * part + h * HEAD_DIM, 2 * part + (h + 1) * HEAD_DIM)
            for count in reversed(range(blocks)):
                allowed = allowed_at(ids, seq, block, count, spans)
                rows = slice(seq * length + count * block, seq * length + (count + 1) * block)
                keys = slice(seq * length, seq * length + (count + 1) * block)
                shares = softmax_parts(query[rows, head], key[keys, head], allowed)
                share_grad = dot_rows(attended_grad[rows, head], value[keys, head])
                inner = jnp.sum(shares * share_grad, axis=1, keepdims=True)
                score_grad = (shares * (share_grad - inner)).astype(BF16)
                raw[rows, head] = dot(score_grad, key[keys, head]) * scale
                key_grad = dot_first(score_grad, query[rows, head]) * scale
                value_grad = dot_first(shares.astype(BF16), attended_grad[rows, head])
                if count == blocks - 1:
                    raw[keys, key_at] = key_grad
                    raw[keys, value_at] = value_grad
                else:
                    raw[keys, key_at] += key_grad
                    raw[keys, value_at] += value_grad

    gain_rows = jnp.zeros((1, 2 * part), F32)

    for i in range(tiles):
        place = slice(i * ROW_TILE % length, i * ROW_TILE % length + ROW_TILE)
        for h in range(2 * part // HEAD_DIM):
            head = slice(h * HEAD_DIM, (h + 1) * HEAD_DIM)
            raw[at(i), head] = turn(raw[at(i), head], cosine[place, :], -sine[place, :])
        terms = raw[at(i), : 2 * part] * normed[at(i), :]
        gain_rows = gain_rows + jnp.sum(terms, axis=0, keepdims=True)
        for n in range(2):
            own[n : n + 1, at(i)] = row_sums((terms * gain)[:, n * part : (n + 1) * part])
        mixed[at(i), 2 * part :] = raw[at(i), 2 * part :].astype(BF16)

    stats.start()
    wide = width // 128
    for n in range(wide):
        column = slice(n * 128, (n + 1) * 128)
        sums[n : n + 1, :] = gain_attn[:, column]
        sums[wide + n : wide + n + 1, :] = gain_feed[:, column]
    for n in range(2 * part // 128):
        sums[2 * wide + n : 2 * wide + n + 1, :] = gain_rows[:, n * 128 : (n + 1) * 128]
    own[...] = stats.total() / width

    @pl.loop(0, tiles)
    def _(i):
        for n in range(2):
            mean, by = down_rows(own[n : n + 1, at(i)]), down_rows(factor[n : n + 1, at(i)])
            for first in range(n * part, (n + 1) * part, 128):
                where = slice(first, first + 128)
                back = gain[:, where] * raw[at(i), where] - normed[at(i), where] * mean
                mixed[at(i), where] = (by * back).astype(BF16)

    load_w.wait()

    @pl.loop(0, tiles)
    def _(i):
        held[at(i), :] = dot_rows(mixed[at(i), :], held_w[...]).astype(BF16)

    load_tokens.wait()

    def work():
        @pl.loop(0, width // ROW_TILE)
        def _(i):
            qkv_part[at(i), :] = dot_first(held_tokens[:, at(i)], mixed[...]).astype(BF16)

    extra.work = work
    extra.late = up_sums.relay if chips == 4 else (lambda: None)
    exchange.body(
        held, residual_grad, qkv_part, sums, out_part, input_grad, grad_qkv, grad_gains, grad_out, *rest
    )
    if chips == 4:
        for half in range(2):
            up_sum[half * half_rows : (half + 1) * half_rows, :] = up_sums.finish(half).astype(BF16)


def attend_back(
    spans, chips, rows, grads, tokens, weights, up_part, out_w, gains, ids, cosine, sine, residual_grad, gain_attn,
    gain_feed, saved,
):
    total_rows, width = tokens.shape
    part = out_w.shape[0]
    members = width // part
    hidden = up_part.shape[1]
    tiles = total_rows // ROW_TILE
    vmem = pl.BlockSpec(memory_space=pltpu.VMEM)
    hbm = pl.BlockSpec(memory_space=pl.ANY)
    shape = jax.ShapeDtypeStruct
    sum_rows = (2 * width + 2 * part) // 128
    sum_rows += -sum_rows % 8
    extra = QkvGrads(
        spans, chips, members, shape((width, 3 * part), BF16), shape((sum_rows, 128), F32), shape((part, width), BF16)
    )
    exchange = Exchange(spans, rows, width, SUM_PIECE, True, False, after_input, 1, 1, None, extra)
    scratch = exchange.scratch()
    square_in = chips == 4
    return pl.pallas_call(
        functools.partial(attend_back_body, spans, chips, exchange, extra, len(scratch) - len(extra.scratch())),
        out_shape=[
            shape((rows, width), F32),
            *extra.out_shapes,
            shape((width // chips, hidden) if square_in else (16, 128), BF16),
        ],
        in_specs=[hbm] * 4 + [vmem] * (8 + len(saved)),
        out_specs=[vmem] * 5,
        scratch_shapes=[
            pltpu.VMEM((total_rows, width), BF16),
            pltpu.VMEM((total_rows, width), BF16),
            pltpu.VMEM(weights.shape, BF16),
            pltpu.VMEM((total_rows, 3 * part), F32),
            pltpu.VMEM((total_rows, 3 * part), BF16),
            pltpu.VMEM((total_rows, part), BF16),
            *stats_scratch(spans, total_rows)[:2],
            pltpu.SemaphoreType.DMA((tiles + 3,)),
            *stats_scratch(spans, total_rows)[2:],
            pltpu.VMEM((width, 3 * part), BF16),
            pltpu.VMEM((part, width), BF16),
            pltpu.VMEM((sum_rows, 128), F32),
            pltpu.VMEM((width, hidden) if square_in else (16, 128), BF16),
            pltpu.VMEM((6, width // 8, hidden) if square_in else (6, 16, 128), BF16),
            pltpu.SemaphoreType.DMA((6,)),
            pltpu.SemaphoreType.DMA((6,)),
            *scratch,
        ],
        compiler_params=pltpu.CompilerParams(collective_id=9, has_side_effects=True, vmem_limit_bytes=62 << 20),
        cost_estimate=pl.CostEstimate(
            flops=2 * total_rows * width * 8 * part, bytes_accessed=50 * width * width, transcendentals=0
        ),
        name="attend_back",
    )(
        grads, tokens, weights, up_part, out_w, gains, ids, cosine, sine, residual_grad, gain_attn, gain_feed, *saved
    )


def per_device(inputs, segment, w_qkv, w_out, w_gate, w_up, w_down_t, gains, cotangent):
    rows, width = inputs.shape[1:]
    cores = lax.axis_size("core")
    spans = lax.axis_size("ctx")
    members = cores * spans
    length = rows * spans
    part = width // members
    tokens = inputs[0]

    qkv_rows = w_qkv.shape[0]
    qkv_cut = w_qkv.reshape(qkv_rows, 3, members, part).transpose(2, 0, 1, 3)
    qkv_cut = qkv_cut.reshape(members, qkv_rows, 3 * part)
    chips = lax.axis_size("chip")
    assert chips == spans
    gate_up, down = split_columns(w_gate, w_up, w_down_t)
    cosine, sine = rope_tables(jnp.arange(length, dtype=F32))
    half = jnp.arange(HEAD_DIM) < HEAD_DIM // 2
    sine = jnp.where(half[None, :], -sine, sine)
    qkv_w, ids, tokens_all, gate_up_w, out_part, out_w, *saved = attend(
        spans, chips, tokens, qkv_cut, jnp.broadcast_to(segment, (8, rows)), w_out, gate_up, gains, cosine, sine
    )
    if chips != 4:
        gate_up_w = gather(gate_up, "chip")
    (
        output, residual_grad, gain_feed, gain_attn, down_sum, gate_sum, _, _, gate_part, up_part, projected_all
    ) = Middle(spans, rows, width, w_gate.shape[1] // cores, BATCH_PIECE).call(
        chips, out_part, tokens, cotangent[0], gains, gate_up, gate_up_w, down
    )
    input_grad, grad_qkv, grad_gains, grad_out, up_sum = attend_back(
        spans, chips, rows, projected_all, tokens_all, qkv_w, up_part, out_w, gains, ids, cosine, sine, residual_grad,
        gain_attn, gain_feed, saved,
    )
    if chips != 4:
        gate_sum, up_sum = scatter_sum(gate_part, "chip"), scatter_sum(up_part, "chip")
    grad_gate, grad_up, grad_down = join_columns(gate_sum, up_sum, down_sum)
    return (
        output[None],
        input_grad[None],
        grad_qkv,
        grad_out,
        grad_gate,
        grad_up,
        grad_down,
        grad_gains.reshape(4, width),
    )


def solution(mesh):
    cores = 2
    chips = mesh.shape["dp"] // cores
    split = Mesh(mesh.devices.reshape(chips, cores, mesh.shape["ctx"]), ALL)
    dp = ("chip", "core")
    every = P((*dp, "ctx"), None)
    in_specs = (
        P(dp, "ctx", None),
        P(dp, "ctx"),
        every,
        every,
        P(dp, "ctx"),
        P(dp, "ctx"),
        P(dp, "ctx"),
        P(),
        P(dp, "ctx", None),
    )
    out_specs = (
        P(dp, "ctx", None),
        P(dp, "ctx", None),
        every,
        every,
        P(dp, "ctx"),
        P(dp, "ctx"),
        P(dp, "ctx"),
        P(),
    )
    return jax.shard_map(
        per_device, mesh=split, in_specs=in_specs, out_specs=out_specs, check_vma=False
    )
```

profile of v0, /device:TPU:0, one launch (start us, length us, event | category | flops | bytes accessed | tf_op | source)
XLA Modules:
  0.0 496.6 jit_solution(5007914569444233162)
XLA Ops:
  0.7 1.3 broadcast_in_dim.25.own_ids
  2.0 1.0 fusion
  3.0 1.0 negate_select_fusion
  3.9 0.2 copy.19
  4.1 1.4 copy.23
  5.5 3.4 reshape.36.cut
  8.9 3.8 split_columns.1
  12.7 1.3 copy-done.6
  14.0 1.0 copy-done.7
  15.0 111.5 %attend.1 = (bf16[2048,768]{1,0:T(8,128)(2,1)}, s32[64,128]{1,0:T(8,128)}, bf16[1024,2048]{1,0:T(8,128)(2,1)}, bf16[2048,2048]{1,0:T(8,128)(2,1)}, bf16[1024,204...) custom-call(bf16[128,2048]{1,0:T(8,128)(2,1)} %bitcast.23, ...), custom_call_target="tpu_custom_call" | custom-call | flops 5368709120 | bytes 209715200 | tf_op jit(solution)/shard_map/attend/pallas_call | solution.py:1800
  126.5 252.6 %feed_forward.1 = (bf16[128,2048]{1,0:T(8,128)(2,1)}, f32[128,2048]{1,0:T(8,128)}, f32[1,2048]{1,0:T(1,128)}, f32[1,2048]{1,0:T(1,128)}, bf16[512,1024]{1,0:T(8,...) custom-call(bf16[1024,2048]{1,0:T(8,128)(2,1)} %get-tuple-element.39, ...), custom_call_target="tpu_custom_call" | custom-call | flops 38654705664 | bytes 419430400 | tf_op jit(solution)/shard_map/feed_forward/pallas_call | solution.py:1504
  379.1 100.2 %attend_back.1 = (f32[128,2048]{1,0:T(8,128)}, f32[64,6144]{1,0:T(8,128)}, f32[4,16,128]{2,1,0:T(8,128)}, f32[64,2048]{1,0:T(8,128)}, bf16[512,1024]{1,0:T(8,128)(2,1)}) custom-call(bf16[1024,2048]{1,0:T(8,128)(2,1)} %get-tuple-element.43.grads, bf16[1024,2048]{1,0:T(8,128)(2,1)} %get-tuple-element.44.tokens, bf16[2048,768]{1,0:T(8,128)(2,1)} %get-tuple-element.45.weights, ...), custom_call_target="tpu_custom_call" | custom-call | flops 8589934592 | bytes 209715200 | tf_op jit(solution)/shard_map/attend_back/pallas_call | solution.py:2002
  479.3 1.4 copy.24
  480.7 1.2 copy-done.4
  481.9 1.2 copy-done.5
  483.2 5.3 %join_columns.1 = (f32[256,2048]{1,0:T(8,128)S(1)}, f32[256,2048]{1,0:T(8,128)S(1)}, f32[256,2048]{1,0:T(8,128)S(1)}) custom-call(bf16[512,1024]{1,0:T(8,128)(2,1)S(1)} %copy-done.4, bf16[512,1024]{1,0:T(8,128)(2,1)S(1)} %copy-done.5, bf16[512,1024]{1,0:T(8,128)(2,1)S(1)} %copy-done.3), custom_call_target="tpu_custom_call" | custom-call | tf_op jit(solution)/shard_map/join_columns/pallas_call | solution.py:523
  488.5 0.8 copy.32
  489.2 1.0 copy.33
  490.2 1.1 copy.34
  491.4 0.3 copy-done.12
  491.6 0.8 copy.35
  492.4 1.3 copy.36
  493.7 1.3 copy.37
  495.1 1.3 copy.38
  (23 shorter events, 0.1 us)
Async XLA Ops:
  0.6 3.3 copy-start.10
  4.1 4.8 copy-start
  4.1 4.8 copy-start.1
  4.1 4.8 copy-start.2
  12.7 1.3 copy-start.6
  14.0 1.0 copy-start.7
  379.1 101.6 %copy-start.3 = (bf16[512,1024]{1,0:T(8,128)(2,1)S(1)}, bf16[512,1024]{1,0:T(8,128)(2,1)}, u32[]{:S(2)}) copy-start(bf16[512,1024]{1,0:T(8,128)(2,1)} %get-tuple-element.63.down) | copy-start | bytes 3145732
  379.1 109.3 %copy-start.11 = (bf16[128,2048]{1,0:T(8,128)(2,1)S(1)}, bf16[128,2048]{1,0:T(8,128)(2,1)}, u32[]{:S(2)}) copy-start(bf16[128,2048]{1,0:T(8,128)(2,1)} %get-tuple-element.42) | copy-start | bytes 1572868
  480.7 1.2 copy-start.4
  481.9 1.2 copy-start.5
  483.2 6.1 %copy-start.9 = (f32[128,2048]{1,0:T(8,128)S(1)}, f32[128,2048]{1,0:T(8,128)}, u32[]{:S(2)}) copy-start(f32[128,2048]{1,0:T(8,128)} %get-tuple-element.58) | copy-start | bytes 3145732
  488.4 1.8 copy-start.8
  490.2 1.4 copy-start.12
where the time goes:
time: 506 us; the launch traced here: 497 us
  Pallas kernels  473 us (93%)
  local copies, waits for them, and re-layouts  20.3 us (4%)
    pallas_call x1, Pallas kernels, call(): pl.pallas_call(functools.partial(self.body, chips), out_shape=[shape((row...  253 us
    pallas_call x1, Pallas kernels, attend(): pl.pallas_call(functools.partial(attend_body, spans, chips, exchange, ext...  112 us
    pallas_call x1, Pallas kernels, attend_back(): pl.pallas_call(functools.partial(attend_back_body, spans, chips, exchange...  100 us
    unnamed x35, local copies, waits for them, and re-layouts  14.2 us

commit v1 on v0

--- a/solution.py
+++ b/solution.py
@@ -427,7 +427,7 @@
     pl.semaphore_wait(barrier, 1)
 
 
-def split_body(gate, up, down, gate_up_out, down_out, held, load_sem, store_sem, send_sem, recv_sem):
+def split_copies(gate, up, down, gate_up_out, down_out, held, load_sem, store_sem, send_sem, recv_sem):
     core = lax.axis_index("core")
     other = 1 - core
     rows, width = gate.shape
@@ -436,46 +436,17 @@
     places = [gate_up_out.at[where, :half], gate_up_out.at[where, half:], down_out.at[where, :]]
     mine = pl.ds(pl.multiple_of(core * half, half), half)
     theirs = pl.ds(pl.multiple_of(other * half, half), half)
-    loads = [
-        pltpu.make_async_copy(a.at[:, mine], held.at[i], load_sem.at[i]) for i, a in enumerate((gate, up, down))
-    ]
-    for load in loads:
-        load.start()
-    meet_other_core()
+    arrays = list(enumerate((gate, up, down)))
+    loads = [pltpu.make_async_copy(a.at[:, mine], held.at[i], load_sem.at[i]) for i, a in arrays]
     sends = [
         pltpu.make_async_remote_copy(
             src_ref=a.at[:, theirs], dst_ref=places[i], send_sem=send_sem.at[i], recv_sem=recv_sem.at[i],
             device_id={"core": other}, device_id_type=MESH_ID,
         )
-        for i, a in enumerate((gate, up, down))
+        for i, a in arrays
     ]
-    for send in sends:
-        send.start()
     stores = [pltpu.make_async_copy(held.at[i], places[i], store_sem.at[i]) for i in range(3)]
-    for load, store in zip(loads, stores):
-        load.wait()
-        store.start()
-    for store, send in zip(stores, sends):
-        store.wait()
-        send.wait()
-
-
-def split_columns(gate, up, down):
-    rows, width = gate.shape
-    hbm = pl.BlockSpec(memory_space=pl.ANY)
-    three = pltpu.SemaphoreType.DMA((3,))
-    return pl.pallas_call(
-        split_body,
-        out_shape=[
-            jax.ShapeDtypeStruct((2 * rows, width), BF16),
-            jax.ShapeDtypeStruct((2 * rows, width // 2), BF16),
-        ],
-        in_specs=[hbm] * 3,
-        out_specs=[hbm] * 2,
-        scratch_shapes=[pltpu.VMEM((3, rows, width // 2), BF16)] + [three] * 4,
-        compiler_params=pltpu.CompilerParams(collective_id=6, has_side_effects=True, vmem_limit_bytes=8 << 20),
-        name="split_columns",
-    )(gate, up, down)
+    return loads, sends, stores
 
 
 def join_body(gate, up, down, gate_out, up_out, down_out, arrived, send_sem, recv_sem):
@@ -691,9 +662,9 @@
         self.sum_rows = sums.shape[0]
         vmem = pl.BlockSpec(memory_space=pltpu.VMEM)
         self.out_shapes = [
-            jax.ShapeDtypeStruct((self.block, 3 * self.width), F32),
+            jax.ShapeDtypeStruct((self.block, 3 * self.width), BF16),
             jax.ShapeDtypeStruct((4, self.width // 128, 128), F32),
-            jax.ShapeDtypeStruct((self.out_rows, self.width), F32),
+            jax.ShapeDtypeStruct((self.out_rows, self.width), BF16),
         ]
         self.out_specs = [vmem] * 3
 
@@ -702,7 +673,7 @@
         chip_sems = pltpu.SemaphoreType.DMA((self.chips,))
         cross = pltpu.SemaphoreType.DMA((self.chips, self.members))
         return [
-            pltpu.VMEM((self.chips, self.members, self.block, self.columns), BF16),
+            pltpu.VMEM((3 if self.chips == 4 else self.chips, self.members, self.block, self.columns), BF16),
             pltpu.VMEM((self.members, self.block, self.columns), BF16),
             pltpu.VMEM((self.members, self.block, self.columns), BF16),
             pltpu.VMEM((self.members, self.block, self.columns), BF16),
@@ -889,13 +860,13 @@
         for m in range(self.members):
             for i in range(3):
                 self.outs[0][:, i * self.width + m * self.part : i * self.width + (m + 1) * self.part] = (
-                    self.columns_in[m, :, i * self.part : (i + 1) * self.part].astype(F32)
+                    self.columns_in[m, :, i * self.part : (i + 1) * self.part]
                 )
         @pl.when(jnp.logical_not(stays(self.chip, self.core, self.place, self.spans)))
         def _():
             self.move_copy().wait()
 
-        self.outs[2][...] = self.out_final[...].astype(F32)
+        self.outs[2][...] = self.out_final[...]
         for s in range(1, self.chips):
             self.sums_chip(s).wait_send()
             self.out_copy(s).wait_send()
@@ -1669,10 +1640,10 @@
 
 def attend_body(
     spans, chips, exchange, extra, n_scratch,
-    tokens, cut, own_ids, w_out, gate_up, gains, cosine, sine,
-    weights_out, ids, tokens_all, gate_up_w,
+    tokens, w_qkv, segment, w_out, w_gate, w_up, w_down, gains, cosine, sine,
+    gate_up, down, weights_out, ids, tokens_all, gate_up_w,
     partial_out, out_w_out, query_out, key_out, value_out, normed_out, factor_out, attended_out,
-    raw, given, out_w, moved, own, arrived, store_sem, chip_send, chip_recv, send, recv, move_send, move_recv,
+    cut, own_ids, split, split_sems, raw, given, out_w, moved, own, arrived, store_sem, chip_send, chip_recv, send, recv, move_send, move_recv,
     up_send, up_recv, *rest,
 ):
     part = out_w.shape[0]
@@ -1707,7 +1678,19 @@
     if chips == 4:
         up = Neighbours(chip, gate_up, gate_up_w, up_send, up_recv)
     own[...] = jnp.zeros_like(own)
+    loads, sends, stores = split_copies(w_gate, w_up, w_down, gate_up, down, split, *(split_sems.at[n] for n in range(4)))
+    for load in loads:
+        load.start()
+    for m in range(2 * spans):
+        for i in range(3):
+            column = i * width + m * part
+            cut[m, :, i * part : (i + 1) * part] = w_qkv[:, column : column + part]
+    own_ids[...] = jnp.broadcast_to(segment[...], own_ids.shape)
     wait_all(spans, True)
+    for load, store, other in zip(loads, stores, sends):
+        other.start()
+        load.wait()
+        store.start()
 
     @pl.when(home)
     def _():
@@ -1725,6 +1708,9 @@
         for s in range(1, chips):
             chip_copy(s).start()
         out_w[here, :] = moved[...]
+        for store, other in zip(stores, sends):
+            store.wait()
+            other.wait()
         if chips == 4:
             up.begin()
 
@@ -1786,7 +1772,7 @@
         up.finish()
 
 
-def attend(spans, chips, tokens, cut, ids, w_out, gate_up, gains, cosine, sine):
+def attend(spans, chips, tokens, w_qkv, segment, w_out, w_gate, w_up, w_down, gains, cosine, sine):
     rows, width = tokens.shape
     total_rows = 2 * spans * rows
     part = w_out.shape[0] * chips
@@ -1794,15 +1780,19 @@
     vmem = pl.BlockSpec(memory_space=pltpu.VMEM)
     hbm = pl.BlockSpec(memory_space=pl.ANY)
     shape = jax.ShapeDtypeStruct
-    extra = QkvWeights(spans, chips, cut, ids)
+    cut = shape((2 * spans, w_qkv.shape[0], 3 * part), BF16)
+    extra = QkvWeights(spans, chips, cut, shape((8, rows), jnp.int32))
+    slab, columns = w_gate.shape
     exchange = Exchange(spans, rows, width, PIECE, False, True, pass_tokens, 1, 0, None, extra)
     scratch = exchange.scratch()
     return pl.pallas_call(
         functools.partial(attend_body, spans, chips, exchange, extra, len(scratch) - len(extra.scratch())),
         out_shape=[
+            shape((2 * slab, columns), BF16),
+            shape((2 * slab, columns // 2), BF16),
             *extra.out_shapes,
             shape((total_rows, width), BF16),
-            shape((chips * gate_up.shape[0] if chips == 4 else 16, gate_up.shape[1]), BF16),
+            shape((chips * 2 * slab if chips == 4 else 16, columns), BF16),
             shape((total_rows, width), BF16),
             shape((part, width), BF16),
             shape((total_rows, part), BF16),
@@ -1812,9 +1802,13 @@
             shape((8, total_rows), F32),
             shape((total_rows, part), BF16),
         ],
-        in_specs=[vmem] * 4 + [hbm] + [vmem] * 3,
-        out_specs=[vmem] * 2 + [hbm] * 3 + [vmem] * 7,
+        in_specs=[vmem] * 4 + [hbm] * 3 + [vmem] * 3,
+        out_specs=[hbm] * 2 + [vmem] * 2 + [hbm] * 3 + [vmem] * 7,
         scratch_shapes=[
+            pltpu.VMEM(cut.shape, BF16),
+            pltpu.VMEM((8, rows), jnp.int32),
+            pltpu.VMEM((3, slab, columns // 2), BF16),
+            pltpu.SemaphoreType.DMA((4, 3)),
             pltpu.VMEM((total_rows, 3 * part), F32),
             pltpu.VMEM((2, ROW_TILE, width), BF16),
             pltpu.VMEM((part, width), BF16),
@@ -1835,16 +1829,16 @@
             flops=2 * total_rows * width * 5 * part, bytes_accessed=50 * width * width, transcendentals=0
         ),
         name="attend",
-    )(tokens, cut, ids, w_out, gate_up, gains, cosine, sine)
+    )(tokens, w_qkv, segment, w_out, w_gate, w_up, w_down, gains, cosine, sine)
 
 
 def attend_back_body(
     spans, chips, exchange, extra, n_scratch,
-    grads, tokens, weights, up_part, out_w, gains, ids, cosine, sine, residual_grad, gain_attn, gain_feed,
+    grads, tokens, weights, up_part, gate_sum, down_sum, out_w, gains, ids, cosine, sine, residual_grad, gain_attn, gain_feed,
     query, key, value, normed, factor, attended,
-    input_grad, grad_qkv, grad_gains, grad_out, up_sum,
+    input_grad, grad_qkv, grad_gains, grad_out, grad_gate, grad_down, grad_up,
     held, held_tokens, held_w, raw, mixed, attended_grad, own, arrived, load_sem, send, recv,
-    qkv_part, out_part, sums, up_held, up_landed, up_send, up_recv, *rest,
+    qkv_part, out_part, sums, up_held, up_landed, up_send, up_recv, joined, join_send, join_recv, *rest,
 ):
     part = out_w.shape[0]
     total_rows = raw.shape[0]
@@ -1899,6 +1893,29 @@
         )
         up_sums.begin(0)
         up_sums.begin(2)
+        slab = gate_sum.shape[0] // 2
+        side = gate_sum.shape[1]
+        my_chip = lax.axis_index("chip")
+        up_sum = up_held.at[pl.ds(pl.multiple_of(my_chip * 2 * slab, 2 * slab), 2 * slab)]
+        pairs = ((gate_sum, grad_gate), (down_sum, grad_down), (up_sum, grad_up))
+        theirs = pl.ds(pl.multiple_of((1 - stats.core) * slab, slab), slab)
+        near = pl.ds(pl.multiple_of(stats.core * side, side), side)
+        far = pl.ds(pl.multiple_of((1 - stats.core) * side, side), side)
+
+        def join_copy(n):
+            return pltpu.make_async_remote_copy(
+                src_ref=pairs[n][0].at[theirs], dst_ref=joined.at[n], send_sem=join_send.at[n],
+                recv_sem=join_recv.at[n], device_id={"core": 1 - stats.core}, device_id_type=MESH_ID,
+            )
+
+        def join(n):
+            given, out = pairs[n]
+            out[:, near] = given[pl.ds(pl.multiple_of(stats.core * slab, slab), slab), :]
+            join_copy(n).wait()
+            out[:, far] = joined[n]
+
+        join_copy(0).start()
+        join_copy(1).start()
     block = QUERY_BLOCK
     blocks = length // block
     for seq in range(2):
@@ -1977,11 +1994,14 @@
     if chips == 4:
         for half in range(2):
             up_sum[half * half_rows : (half + 1) * half_rows, :] = up_sums.finish(half).astype(BF16)
+        join_copy(2).start()
+        for n in range(3):
+            join(n)
 
 
 def attend_back(
-    spans, chips, rows, grads, tokens, weights, up_part, out_w, gains, ids, cosine, sine, residual_grad, gain_attn,
-    gain_feed, saved,
+    spans, chips, rows, grads, tokens, weights, up_part, gate_sum, down_sum, out_w, gains, ids, cosine, sine,
+    residual_grad, gain_attn, gain_feed, saved,
 ):
     total_rows, width = tokens.shape
     part = out_w.shape[0]
@@ -2004,10 +2024,10 @@
         out_shape=[
             shape((rows, width), F32),
             *extra.out_shapes,
-            shape((width // chips, hidden) if square_in else (16, 128), BF16),
+            *[shape((width // chips // 2, 2 * hidden) if square_in else (16, 128), BF16)] * 3,
         ],
-        in_specs=[hbm] * 4 + [vmem] * (8 + len(saved)),
-        out_specs=[vmem] * 5,
+        in_specs=[hbm] * 4 + [vmem] * (10 + len(saved)),
+        out_specs=[vmem] * 7,
         scratch_shapes=[
             pltpu.VMEM((total_rows, width), BF16),
             pltpu.VMEM((total_rows, width), BF16),
@@ -2025,6 +2045,9 @@
             pltpu.VMEM((6, width // 8, hidden) if square_in else (6, 16, 128), BF16),
             pltpu.SemaphoreType.DMA((6,)),
             pltpu.SemaphoreType.DMA((6,)),
+            pltpu.VMEM((3, width // chips // 2, hidden) if square_in else (3, 16, 128), BF16),
+            pltpu.SemaphoreType.DMA((3,)),
+            pltpu.SemaphoreType.DMA((3,)),
             *scratch,
         ],
         compiler_params=pltpu.CompilerParams(collective_id=9, has_side_effects=True, vmem_limit_bytes=62 << 20),
@@ -2033,7 +2056,8 @@
         ),
         name="attend_back",
     )(
-        grads, tokens, weights, up_part, out_w, gains, ids, cosine, sine, residual_grad, gain_attn, gain_feed, *saved
+        grads, tokens, weights, up_part, gate_sum, down_sum, out_w, gains, ids, cosine, sine, residual_grad, gain_attn,
+        gain_feed, *saved,
     )
 
 
@@ -2046,17 +2070,13 @@
     part = width // members
     tokens = inputs[0]
 
-    qkv_rows = w_qkv.shape[0]
-    qkv_cut = w_qkv.reshape(qkv_rows, 3, members, part).transpose(2, 0, 1, 3)
-    qkv_cut = qkv_cut.reshape(members, qkv_rows, 3 * part)
     chips = lax.axis_size("chip")
     assert chips == spans
-    gate_up, down = split_columns(w_gate, w_up, w_down_t)
     cosine, sine = rope_tables(jnp.arange(length, dtype=F32))
     half = jnp.arange(HEAD_DIM) < HEAD_DIM // 2
     sine = jnp.where(half[None, :], -sine, sine)
-    qkv_w, ids, tokens_all, gate_up_w, out_part, out_w, *saved = attend(
-        spans, chips, tokens, qkv_cut, jnp.broadcast_to(segment, (8, rows)), w_out, gate_up, gains, cosine, sine
+    gate_up, down, qkv_w, ids, tokens_all, gate_up_w, out_part, out_w, *saved = attend(
+        spans, chips, tokens, w_qkv, segment, w_out, w_gate, w_up, w_down_t, gains, cosine, sine
     )
     if chips != 4:
         gate_up_w = gather(gate_up, "chip")
@@ -2065,21 +2085,21 @@
     ) = Middle(spans, rows, width, w_gate.shape[1] // cores, BATCH_PIECE).call(
         chips, out_part, tokens, cotangent[0], gains, gate_up, gate_up_w, down
     )
-    input_grad, grad_qkv, grad_gains, grad_out, up_sum = attend_back(
-        spans, chips, rows, projected_all, tokens_all, qkv_w, up_part, out_w, gains, ids, cosine, sine, residual_grad,
+    input_grad, grad_qkv, grad_gains, grad_out, grad_gate, grad_down, grad_up = attend_back(
+        spans, chips, rows, projected_all, tokens_all, qkv_w, up_part, gate_sum, down_sum, out_w, gains, ids, cosine, sine, residual_grad,
         gain_attn, gain_feed, saved,
     )
     if chips != 4:
         gate_sum, up_sum = scatter_sum(gate_part, "chip"), scatter_sum(up_part, "chip")
-    grad_gate, grad_up, grad_down = join_columns(gate_sum, up_sum, down_sum)
+        grad_gate, grad_up, grad_down = join_columns(gate_sum, up_sum, down_sum)
     return (
         output[None],
         input_grad[None],
-        grad_qkv,
-        grad_out,
-        grad_gate,
-        grad_up,
-        grad_down,
+        grad_qkv.astype(F32),
+        grad_out.astype(F32),
+        grad_gate.astype(F32),
+        grad_up.astype(F32),
+        grad_down.astype(F32),
         grad_gains.reshape(4, width),
     )
 

time: 506 us -> 494 us (0.976)
  local copies, waits for them, and re-layouts: 20.3 us -> 3.25 us
  other arithmetic: 1.97 us -> 12.2 us
    unnamed x35 -> x11, local copies, waits for them, and re-layouts: 14.2 us -> 3.25 us
    convert_element_type x0 -> x5, other arithmetic: none -> 10.2 us  [the longest x1 2.85 us: per_device(): grad_gate.astype(F32)]
    pallas_call x2 -> x0, Pallas kernels: 9.03 us -> none  [the longest x1 5.26 us: join_columns(): pl.pallas_call(join_body, out_shape=[jax.ShapeDtypeStruct((rows, 2 * half...]
where the time goes in v1:
time: 494 us; the launch traced here: 486 us
  Pallas kernels  469 us (95%)
  other arithmetic  12.2 us (2%)
    pallas_call x1, Pallas kernels, call(): pl.pallas_call(functools.partial(self.body, chips), out_shape=[shape((row...  252 us
    pallas_call x1, Pallas kernels, attend(): pl.pallas_call(functools.partial(attend_body, spans, chips, exchange, ext...  112 us
    pallas_call x1, Pallas kernels, attend_back(): pl.pallas_call(functools.partial(attend_back_body, spans, chips, exchange...  105 us

profile of v1, /device:TPU:0, one launch (start us, length us, event | category | flops | bytes accessed | tf_op | source)
XLA Modules:
  0.0 485.6 jit_solution(7297754569004326589)
XLA Ops:
  0.7 1.0 fusion
  1.6 1.0 negate_select_fusion
  2.6 111.7 %attend.1 = (bf16[512,2048]{1,0:T(8,128)(2,1)}, bf16[512,1024]{1,0:T(8,128)(2,1)}, bf16[2048,768]{1,0:T(8,128)(2,1)}, s32[64,128]{1,0:T(8,128)}, bf16[1024,2048]...) custom-call(bf16[128,2048]{1,0:T(8,128)(2,1)} %bitcast.12, ...), custom_call_target="tpu_custom_call" | custom-call | flops 5368709120 | bytes 209715200 | tf_op jit(solution)/shard_map/attend/pallas_call | solution.py:1788
  114.3 252.4 %feed_forward.1 = (bf16[128,2048]{1,0:T(8,128)(2,1)}, f32[128,2048]{1,0:T(8,128)}, f32[1,2048]{1,0:T(1,128)}, f32[1,2048]{1,0:T(1,128)}, bf16[512,1024]{1,0:T(8,...) custom-call(bf16[1024,2048]{1,0:T(8,128)(2,1)} %get-tuple-element.37, ...), custom_call_target="tpu_custom_call" | custom-call | flops 38654705664 | bytes 419430400 | tf_op jit(solution)/shard_map/feed_forward/pallas_call | solution.py:1475
  366.8 105.2 %attend_back.1 = (f32[128,2048]{1,0:T(8,128)}, bf16[64,6144]{1,0:T(8,128)(2,1)}, f32[4,16,128]{2,1,0:T(8,128)}, bf16[64,2048]{1,0:T(8,128)(2,1)}, bf16[256,2048]...) custom-call(bf16[1024,2048]{1,0:T(8,128)(2,1)} %get-tuple-element.42.grads, ...), custom_call_target="tpu_custom_call" | custom-call | flops 8589934592 | bytes 209715200 | tf_op jit(solution)/shard_map/attend_back/pallas_call | solution.py:2022
  471.9 0.0 copy-start.1
  472.0 1.5 copy.19
  473.4 1.8 convert_element_type.16
  475.2 0.0 copy-start
  475.2 2.5 convert_element_type.15
  477.7 0.0 copy-start.3
  477.7 2.8 convert_element_type.17
  480.5 0.0 copy-done.1
  480.5 0.0 copy-start.2
  480.5 1.6 convert_element_type.18
  482.1 0.0 copy-done
  482.1 1.6 convert_element_type.19
  483.7 0.0 copy-done.3
  483.7 0.8 copy.22
  484.4 0.0 copy-done.2
  484.5 1.0 copy.23
  (2 shorter events, 0.0 us)
Async XLA Ops:
  471.9 8.6 %copy-start.1 = (bf16[256,2048]{1,0:T(8,128)(2,1)S(1)}, bf16[256,2048]{1,0:T(8,128)(2,1)}, u32[]{:S(2)}) copy-start(bf16[256,2048]{1,0:T(8,128)(2,1)} %get-tuple-element.63) | copy-start | bytes 3145732
  475.2 6.9 %copy-start = (bf16[256,2048]{1,0:T(8,128)(2,1)S(1)}, bf16[256,2048]{1,0:T(8,128)(2,1)}, u32[]{:S(2)}) copy-start(bf16[256,2048]{1,0:T(8,128)(2,1)} %get-tuple-element.64) | copy-start | bytes 3145732
  477.7 6.0 %copy-start.3 = (bf16[128,2048]{1,0:T(8,128)(2,1)S(1)}, bf16[128,2048]{1,0:T(8,128)(2,1)}, u32[]{:S(2)}) copy-start(bf16[128,2048]{1,0:T(8,128)(2,1)} %get-tuple-element.41) | copy-start | bytes 1572868
  480.5 3.9 copy-start.2

commit v2 on v1

--- a/solution.py
+++ b/solution.py
@@ -1404,7 +1404,7 @@
                     give(seq, d, k).wait()
             spread_sent(k)
 
-        step = 2 * last + 2
+        step = 2 * last + 3
         last_steps = 9 if chips == 4 else chips + down_tiles // 2
         assert last_steps <= step + 1
 

time: 494 us -> 494 us (level)
  no operation moved by 1% of the time
where the time goes in v2:
time: 494 us; the launch traced here: 485 us
  Pallas kernels  469 us (95%)
  other arithmetic  12.2 us (2%)
    pallas_call x1, Pallas kernels, call(): pl.pallas_call(functools.partial(self.body, chips), out_shape=[shape((row...  253 us
    pallas_call x1, Pallas kernels, attend(): pl.pallas_call(functools.partial(attend_body, spans, chips, exchange, ext...  112 us
    pallas_call x1, Pallas kernels, attend_back(): pl.pallas_call(functools.partial(attend_back_body, spans, chips, exchange...  105 us

profile of v2, /device:TPU:0, one launch (start us, length us, event | category | flops | bytes accessed | tf_op | source)
XLA Modules:
  0.0 485.5 jit_solution(8470804414501251179)
XLA Ops:
  0.7 1.0 fusion
  1.6 1.0 negate_select_fusion
  2.6 111.7 %attend.1 = (bf16[512,2048]{1,0:T(8,128)(2,1)}, bf16[512,1024]{1,0:T(8,128)(2,1)}, bf16[2048,768]{1,0:T(8,128)(2,1)}, s32[64,128]{1,0:T(8,128)}, bf16[1024,2048]...) custom-call(bf16[128,2048]{1,0:T(8,128)(2,1)} %bitcast.12, ...), custom_call_target="tpu_custom_call" | custom-call | flops 5368709120 | bytes 209715200 | tf_op jit(solution)/shard_map/attend/pallas_call | solution.py:1788
  114.3 252.5 %feed_forward.1 = (bf16[128,2048]{1,0:T(8,128)(2,1)}, f32[128,2048]{1,0:T(8,128)}, f32[1,2048]{1,0:T(1,128)}, f32[1,2048]{1,0:T(1,128)}, bf16[512,1024]{1,0:T(8,...) custom-call(bf16[1024,2048]{1,0:T(8,128)(2,1)} %get-tuple-element.37, ...), custom_call_target="tpu_custom_call" | custom-call | flops 38654705664 | bytes 419430400 | tf_op jit(solution)/shard_map/feed_forward/pallas_call | solution.py:1475
  366.9 104.9 %attend_back.1 = (f32[128,2048]{1,0:T(8,128)}, bf16[64,6144]{1,0:T(8,128)(2,1)}, f32[4,16,128]{2,1,0:T(8,128)}, bf16[64,2048]{1,0:T(8,128)(2,1)}, bf16[256,2048]...) custom-call(bf16[1024,2048]{1,0:T(8,128)(2,1)} %get-tuple-element.42.grads, ...), custom_call_target="tpu_custom_call" | custom-call | flops 8589934592 | bytes 209715200 | tf_op jit(solution)/shard_map/attend_back/pallas_call | solution.py:2022
  471.8 0.0 copy-start.1
  471.8 1.5 copy.19
  473.3 1.8 convert_element_type.16
  475.1 0.0 copy-start
  475.1 2.5 convert_element_type.15
  477.5 0.0 copy-start.3
  477.6 2.8 convert_element_type.17
  480.4 0.0 copy-done.1
  480.4 0.0 copy-start.2
  480.4 1.6 convert_element_type.18
  482.0 0.0 copy-done
  482.0 1.6 convert_element_type.19
  483.5 0.0 copy-done.3
  483.5 0.8 copy.22
  484.3 0.0 copy-done.2
  484.3 1.0 copy.23
  (2 shorter events, 0.0 us)
Async XLA Ops:
  471.8 8.6 %copy-start.1 = (bf16[256,2048]{1,0:T(8,128)(2,1)S(1)}, bf16[256,2048]{1,0:T(8,128)(2,1)}, u32[]{:S(2)}) copy-start(bf16[256,2048]{1,0:T(8,128)(2,1)} %get-tuple-element.63) | copy-start | bytes 3145732
  475.1 6.9 %copy-start = (bf16[256,2048]{1,0:T(8,128)(2,1)S(1)}, bf16[256,2048]{1,0:T(8,128)(2,1)}, u32[]{:S(2)}) copy-start(bf16[256,2048]{1,0:T(8,128)(2,1)} %get-tuple-element.64) | copy-start | bytes 3145732
  477.5 6.0 %copy-start.3 = (bf16[128,2048]{1,0:T(8,128)(2,1)S(1)}, bf16[128,2048]{1,0:T(8,128)(2,1)}, u32[]{:S(2)}) copy-start(bf16[128,2048]{1,0:T(8,128)(2,1)} %get-tuple-element.41) | copy-start | bytes 1572868
  480.4 3.9 copy-start.2
